TPU v7x, 32 devices: a whole 2x2x4 slice. The times are simulated.
32 devices in a mesh: band: 4 (over x, core), grid: 8 (over z, y).
Axes of the slice: x: 2, y: 2, z: 4, core: 2. Of those that a mesh axis runs over, the one named last changes fastest.
Arguments:
- orbitals: float32 [4, 128, 128, 128], P('band', 'grid'), may hold values from -4 to 10, as said below
- pivots: int32 [4], replicated, may hold values from 0 to 2097151, as said below
- pattern: int32 [4, 4], replicated, may hold values from 0 to 1, as said below
Outputs:
- localized: float32 [4, 128, 128, 128], P('band', 'grid')
- exchange_term: float32 [4, 128, 128, 128], P('band', 'grid')
Inputs may be any that keep to these rules, and one draw needn't show every extreme that they name: Values of the orbitals on the grid; the matrix of their values at the pivots has a Cholesky factorization. `pivots`: distinct flat cell indices; the first and the last cell of the grid are always among them. `pattern`: every diagonal entry is 1; each row holds 1 to 4 ones, some row exactly 4; the matrix holds exactly 8 ones.
All inputs are finite; a program needn't handle non-finite values.
Results may differ from a plain program's by a relative error of at most 0.0003.
Values sent between devices are 32-bit elements; how exact they have to be, the bound alone decides.
A program may use at most 64 MiB of HBM per device.

v0:
```python
import jax
import jax.numpy as jnp
from jax import lax
from jax.sharding import PartitionSpec as P

MOST_PARTNERS = 4


precise = lax.Precision.HIGHEST


def tables(length):
    across = jnp.arange(length, dtype=jnp.int32)
    phases = across[:, None] * across[None, :] % length
    angles = phases.astype(jnp.float32) * (2.0 * jnp.pi / length)
    return (jnp.cos(angles), jnp.sin(angles))


def wrapped(indices, length):
    return jnp.where(indices < length // 2, indices, indices - length)


def coulomb(length, plane_start, plane_count):
    wave_first = wrapped(jnp.arange(length, dtype=jnp.int32), length).astype(jnp.float32)
    wave_second = wrapped(plane_start + jnp.arange(plane_count, dtype=jnp.int32), length).astype(
        jnp.float32
    )
    squared = (
        wave_first[:, None, None] ** 2
        + wave_second[None, :, None] ** 2
        + wave_first[None, None, :] ** 2
    )
    scaling = float(length) ** 1.5
    return jnp.where(squared > 0, 0.25 / (scaling * jnp.maximum(squared, 1.0)), 0.0)


def densities(first_bands, second_bands):
    return (first_bands[:, None] * second_bands[None, :]).reshape((-1,) + first_bands.shape[1:])


def applied(potential, first_bands, second_bands):
    shaped = potential.reshape(
        (first_bands.shape[0], second_bands.shape[0]) + first_bands.shape[1:]
    )
    return jnp.sum(shaped * second_bands[None], axis=1)


def filtered(real_in, imag_in, kernel, cos_table, sin_table):
    real_part = jnp.dot(real_in, cos_table, precision=precise) + jnp.dot(
        imag_in, sin_table, precision=precise
    )
    imag_part = jnp.dot(imag_in, cos_table, precision=precise) - jnp.dot(
        real_in, sin_table, precision=precise
    )
    real_part, imag_part = (
        jnp.einsum("pxyz,yk->pxkz", real_part, cos_table, precision=precise)
        + jnp.einsum("pxyz,yk->pxkz", imag_part, sin_table, precision=precise),
        jnp.einsum("pxyz,yk->pxkz", imag_part, cos_table, precision=precise)
        - jnp.einsum("pxyz,yk->pxkz", real_part, sin_table, precision=precise),
    )
    real_wide = lax.all_to_all(real_part, "grid", split_axis=2, concat_axis=1, tiled=True)
    imag_wide = lax.all_to_all(imag_part, "grid", split_axis=2, concat_axis=1, tiled=True)
    ahead_real = (
        jnp.einsum("pxyz,xk->pkyz", real_wide, cos_table, precision=precise)
        + jnp.einsum("pxyz,xk->pkyz", imag_wide, sin_table, precision=precise)
    ) * kernel
    ahead_imag = (
        jnp.einsum("pxyz,xk->pkyz", imag_wide, cos_table, precision=precise)
        - jnp.einsum("pxyz,xk->pkyz", real_wide, sin_table, precision=precise)
    ) * kernel
    back_real = jnp.einsum("pxyz,xk->pkyz", ahead_real, cos_table, precision=precise) - jnp.einsum(
        "pxyz,xk->pkyz", ahead_imag, sin_table, precision=precise
    )
    back_imag = jnp.einsum("pxyz,xk->pkyz", ahead_imag, cos_table, precision=precise) + jnp.einsum(
        "pxyz,xk->pkyz", ahead_real, sin_table, precision=precise
    )
    real_part = lax.all_to_all(back_real, "grid", split_axis=1, concat_axis=2, tiled=True)
    imag_part = lax.all_to_all(back_imag, "grid", split_axis=1, concat_axis=2, tiled=True)
    real_part, imag_part = (
        jnp.einsum("pxyz,yk->pxkz", real_part, cos_table, precision=precise)
        - jnp.einsum("pxyz,yk->pxkz", imag_part, sin_table, precision=precise),
        jnp.einsum("pxyz,yk->pxkz", imag_part, cos_table, precision=precise)
        + jnp.einsum("pxyz,yk->pxkz", real_part, sin_table, precision=precise),
    )
    out_real = jnp.dot(real_part, cos_table, precision=precise) - jnp.dot(
        imag_part, sin_table, precision=precise
    )
    out_imag = jnp.dot(imag_part, cos_table, precision=precise) + jnp.dot(
        real_part, sin_table, precision=precise
    )
    return (out_real, out_imag)


def twin_potential(first_one, second_one, first_two, second_two, kernel, cos_table, sin_table):
    potential_one, potential_two = filtered(
        densities(first_one, second_one),
        densities(first_two, second_two),
        kernel,
        cos_table,
        sin_table,
    )
    return (
        applied(potential_one, first_one, second_one),
        applied(potential_two, first_two, second_two),
    )


def collect(wanted, portion):
    positions = jnp.arange(portion.shape[0], dtype=jnp.int32)
    chooser = (wanted[:, None] == positions[None, :]).astype(jnp.float32)
    return jnp.einsum("qm,mxyz->qxyz", chooser, portion, precision=precise)


def local(orbitals, pivots, pattern):
    band_dev = orbitals.shape[0]
    slab_planes = orbitals.shape[1]
    length = orbitals.shape[3]
    block_total = pattern.shape[0]
    grid_index = lax.axis_index("grid")
    band_index = lax.axis_index("band")
    cell_count = slab_planes * length * length
    flat_local = orbitals.reshape(band_dev, cell_count)
    local_cell = pivots - grid_index * cell_count
    inside = (local_cell >= 0) & (local_cell < cell_count)
    sampled = jnp.take(flat_local, jnp.clip(local_cell, 0, cell_count - 1), axis=1)
    partial_pick = jnp.where(inside[None, :], sampled, 0.0)
    own_rows = lax.psum(partial_pick, "grid")
    picked = lax.all_gather(own_rows, "band", axis=0, tiled=True)
    gram_matrix = jnp.dot(picked.T, picked, precision=precise)
    factor = jnp.linalg.cholesky(gram_matrix)
    rotation = lax.linalg.triangular_solve(factor, picked.T, left_side=True, lower=True).T
    own_weights = lax.dynamic_slice_in_dim(rotation, band_index * band_dev, band_dev, 0)
    localized = lax.psum_scatter(
        jnp.einsum("bk,bxyz->kxyz", own_weights, orbitals, precision=precise),
        "band",
        scatter_dimension=0,
        tiled=True,
    )
    cos_table, sin_table = tables(length)
    plane_count = length // lax.axis_size("grid")
    kernel = coulomb(length, grid_index * plane_count, plane_count)
    columns = jnp.arange(block_total, dtype=jnp.int32)
    members = jnp.arange(band_dev, dtype=jnp.int32)
    own_row = lax.dynamic_index_in_dim(pattern, band_index, 0, keepdims=False)
    before = jnp.cumsum(own_row) - own_row
    slot_ids = jnp.arange(MOST_PARTNERS, dtype=jnp.int32)
    matches = (own_row[None, :] == 1) & (before[None, :] == slot_ids[:, None])
    partner = jnp.sum(jnp.where(matches, columns[None, :], 0), axis=1)
    present = jnp.any(matches, axis=1)
    wanted = jnp.where(
        present[:, None], partner[:, None] * band_dev + members[None, :], -1
    ).reshape(-1)
    partners = collect(wanted, lax.all_gather(localized, "band", axis=0, tiled=True))
    exchange_term = jnp.zeros_like(localized)
    for couple in range(MOST_PARTNERS // 2):
        first_rows = partners[2 * couple * band_dev : (2 * couple + 1) * band_dev]
        second_rows = partners[(2 * couple + 1) * band_dev : (2 * couple + 2) * band_dev]
        term_one, term_two = twin_potential(
            localized, first_rows, localized, second_rows, kernel, cos_table, sin_table
        )
        exchange_term = exchange_term + term_one + term_two
    return (localized, exchange_term)


def solution(mesh):
    return jax.shard_map(
        local,
        mesh=mesh,
        in_specs=(P("band", "grid", None, None), P(), P()),
        out_specs=(P("band", "grid", None, None), P("band", "grid", None, None)),
        check_vma=False,
    )
```

profile of v0, /device:TPU:0, one launch (start us, length us, event | category | flops | bytes accessed | tf_op | source)
XLA Modules:
  0.0 410.2 jit_solution(14240325148722384985)
XLA Ops:
  10.0 23.1 %psum.7 = f32[1,4]{1,0:T(1,128)S(1)} all-reduce(f32[1,4]{1,0:T(1,128)S(1)} %fusion.210), channel_id=1, replica_groups=mesh['band'=4,'grid'=8] {'grid'}, use_global_device_ids=true, to_apply=%region_0.1 | all-reduce | flops 4 | bytes 32 | tf_op jit(solution)/shard_map/psum | solution.py:127
  33.1 5.0 %all-gather = f32[4,1,4]{2,1,0:T(1,128)S(1)} all-gather(f32[1,1,4]{2,1,0:T(1,128)S(1)} %bitcast.338), channel_id=1, replica_groups=mesh['band'=4,'grid'=8] {'band'}, dimensions={0}, use_global_device_ids=true | all-gather | bytes 80 | tf_op jit(solution)/shard_map/all_gather | solution.py:128
  40.6 3.8 broadcast_multiply_fusion
  44.4 41.9 %reduce-scatter.2.cloned.1.call-done = f32[1,16,128,128]{3,2,1,0:T(8,128)} async-done(((f32[4,16,128,128]{3,2,1,0:T(8,128)}), f32[1,16,128,128]{3,2,1,0:T(8,128)}) %reduce-scatter.2.cloned.1.call-update) | async-done | bytes 1048592 | tf_op jit(solution)/shard_map/reduce_scatter | solution.py:133
  87.4 35.6 %all-gather.3.cloned.1.call-done = f32[4,16,128,128]{3,2,1,0:T(8,128)} async-done(((f32[1,16,128,128]{3,2,1,0:T(8,128)}), f32[4,16,128,128]{3,2,1,0:T(8,128)}) %all-gather.3.cloned.1.call-update) | async-done | bytes 4194320 | tf_op jit(solution)/shard_map/all_gather | solution.py:153
  123.0 8.5 %fusion = f32[4,16,128,128]{3,0,2,1:T(4,128)S(1)} fusion(f32[4,16,128,128]{3,2,1,0:T(8,128)} %all-gather.3.cloned.1.call-done, s32[4]{0:T(128)S(1)} %broadcast_select_fusion), kind=kOutput, calls=%fused_computation.1 | convolution fusion | flops 50331664 | bytes 8388624 | tf_op jit(solution)/shard_map/qm,mxyz->qxyz/dot_general | solution.py:111
  131.6 3.8 slice_multiply_fusion.3
  145.5 5.7 %all-to-all-start.4 = ((f32[1,16,128,128]{3,1,0,2:T(8,128)}), f32[1,16,128,128]{3,1,0,2:T(8,128)}, u32[]{:S(2)}, u32[]{:S(2)}) async-start(f32[1,16,128,128]{3,1,0,2:T(8,128)} %copy.182), calls=%async_computation.5 | async-start | bytes 2097152 | tf_op jit(solution)/shard_map/all_to_all | solution.py:61
  156.6 20.8 %all-to-all-done.4 = f32[1,16,128,128]{3,1,0,2:T(8,128)} async-done(((f32[1,16,128,128]{3,1,0,2:T(8,128)}), f32[1,16,128,128]{3,1,0,2:T(8,128)}, u32[]{:S(2)}, u32[]{:S(2)}) %all-to-all-start.4) | async-done | bytes 1048608 | tf_op jit(solution)/shard_map/all_to_all | solution.py:61
  177.4 4.2 %all-to-all-start.5 = ((f32[1,16,128,128]{3,1,0,2:T(8,128)}), f32[1,16,128,128]{3,1,0,2:T(8,128)}, u32[]{:S(2)}, u32[]{:S(2)}) async-start(f32[1,16,128,128]{3,1,0,2:T(8,128)} %copy.187), calls=%async_computation.6 | async-start | bytes 2097152 | tf_op jit(solution)/shard_map/all_to_all | solution.py:62
  190.7 16.6 %all-to-all-done.5 = f32[1,16,128,128]{3,1,0,2:T(8,128)} async-done(((f32[1,16,128,128]{3,1,0,2:T(8,128)}), f32[1,16,128,128]{3,1,0,2:T(8,128)}, u32[]{:S(2)}, u32[]{:S(2)}) %all-to-all-start.5) | async-done | bytes 1048608 | tf_op jit(solution)/shard_map/all_to_all | solution.py:62
  207.3 3.8 all-to-all-start.1
  215.3 21.6 %all-to-all-done.1 = f32[1,16,128,128]{3,1,0,2:T(8,128)S(1)} async-done(((f32[1,16,128,128]{3,1,0,2:T(8,128)}), f32[1,16,128,128]{3,1,0,2:T(8,128)S(1)}, u32[]{:S(2)}, u32[]{:S(2)}) %all-to-all-start.1) | async-done | bytes 1048608 | tf_op jit(solution)/shard_map/all_to_all | solution.py:62
  236.9 3.6 all-to-all-start
  253.0 13.5 %all-to-all-done = f32[1,16,128,128]{3,1,0,2:T(8,128)S(1)} async-done(((f32[1,16,128,128]{3,1,0,2:T(8,128)}), f32[1,16,128,128]{3,1,0,2:T(8,128)S(1)}, u32[]{:S(2)}, u32[]{:S(2)}) %all-to-all-start) | async-done | bytes 1048608 | tf_op jit(solution)/shard_map/all_to_all | solution.py:61
  267.4 4.1 %all-to-all-start.6 = ((f32[1,128,16,128]{3,2,0,1:T(8,128)}), f32[1,128,16,128]{3,2,0,1:T(8,128)S(1)}, u32[]{:S(2)}, u32[]{:S(2)}) async-start(f32[1,128,16,128]{3,2,0,1:T(8,128)} %copy.194), calls=%async_computation.7 | async-start | bytes 2097152 | tf_op jit(solution)/shard_map/all_to_all | solution.py:77
  275.7 21.8 %all-to-all-done.6 = f32[1,128,16,128]{3,2,0,1:T(8,128)S(1)} async-done(((f32[1,128,16,128]{3,2,0,1:T(8,128)}), f32[1,128,16,128]{3,2,0,1:T(8,128)S(1)}, u32[]{:S(2)}, u32[]{:S(2)}) %all-to-all-start.6) | async-done | bytes 1048608 | tf_op jit(solution)/shard_map/all_to_all | solution.py:77
  297.5 4.2 %all-to-all-start.7 = ((f32[1,128,16,128]{3,2,0,1:T(8,128)}), f32[1,128,16,128]{3,2,0,1:T(8,128)}, u32[]{:S(2)}, u32[]{:S(2)}) async-start(f32[1,128,16,128]{3,2,0,1:T(8,128)} %copy.199), calls=%async_computation.8 | async-start | bytes 2097152 | tf_op jit(solution)/shard_map/all_to_all | solution.py:78
  311.7 15.6 %all-to-all-done.7 = f32[1,128,16,128]{3,2,0,1:T(8,128)} async-done(((f32[1,128,16,128]{3,2,0,1:T(8,128)}), f32[1,128,16,128]{3,2,0,1:T(8,128)}, u32[]{:S(2)}, u32[]{:S(2)}) %all-to-all-start.7) | async-done | bytes 1048608 | tf_op jit(solution)/shard_map/all_to_all | solution.py:78
  327.4 4.4 %all-to-all-start.3 = ((f32[1,128,16,128]{3,2,0,1:T(8,128)}), f32[1,128,16,128]{3,2,0,1:T(8,128)}, u32[]{:S(2)}, u32[]{:S(2)}) async-start(f32[1,128,16,128]{3,2,0,1:T(8,128)} %copy.173), calls=%async_computation.4 | async-start | bytes 2097152 | tf_op jit(solution)/shard_map/all_to_all | solution.py:78
  339.7 17.5 %all-to-all-done.3 = f32[1,128,16,128]{3,2,0,1:T(8,128)} async-done(((f32[1,128,16,128]{3,2,0,1:T(8,128)}), f32[1,128,16,128]{3,2,0,1:T(8,128)}, u32[]{:S(2)}, u32[]{:S(2)}) %all-to-all-start.3) | async-done | bytes 1048608 | tf_op jit(solution)/shard_map/all_to_all | solution.py:78
  357.2 4.2 %all-to-all-start.2 = ((f32[1,128,16,128]{3,2,0,1:T(8,128)}), f32[1,128,16,128]{3,2,0,1:T(8,128)}, u32[]{:S(2)}, u32[]{:S(2)}) async-start(f32[1,128,16,128]{3,2,0,1:T(8,128)} %copy.168), calls=%async_computation.3 | async-start | bytes 2097152 | tf_op jit(solution)/shard_map/all_to_all | solution.py:77
  371.7 15.2 %all-to-all-done.2 = f32[1,128,16,128]{3,2,0,1:T(8,128)} async-done(((f32[1,128,16,128]{3,2,0,1:T(8,128)}), f32[1,128,16,128]{3,2,0,1:T(8,128)}, u32[]{:S(2)}, u32[]{:S(2)}) %all-to-all-start.2) | async-done | bytes 1048608 | tf_op jit(solution)/shard_map/all_to_all | solution.py:77
  398.6 4.5 %multiply_add_fusion = f32[1,16,128,128]{3,0,2,1:T(1,128)} fusion(f32[1,16,128,128]{3,0,2,1:T(1,128)S(1)} %bitcast.318, f32[1,16,128,128]{3,0,2,1:T(1,128)S(1)} %bitcast.317, f32[1,16,128,128]{3,0,2,1:T(1,128)S(1)} %bitcast.319, f32[1,16,128,128]{3,0,2,1:T(1,128)S(1)} %bitcast.320, f32[4,16,128,128]{3,0,2,1:T(4,128)S(1)} %copy-done.1), kind=kLoop, calls=%fused_computation.49 | loop fusion | flops 1835008 | bytes 9437184 | tf_op jit(solution)/shard_map/add | solution.py:161
  (109 shorter events, 92.2 us)
Async XLA Ops:
  7.2 79.1 %reduce-scatter.2.cloned.1.call-start = ((), (), s32[]{:S(2)}) async-start(), calls=%async_computation.9 | async-start | bytes 5242880 | tf_op jit(solution)/shard_map/reduce_scatter | solution.py:133
  44.4 78.6 %all-gather.3.cloned.1.call-start = ((), (), s32[]{:S(2)}) async-start(), calls=%async_computation.10 | async-start | bytes 5242880 | tf_op jit(solution)/shard_map/all_gather | solution.py:153
  87.4 44.1 %copy-start.3 = (f32[1,16,128,128]{3,2,1,0:T(8,128)S(1)}, f32[1,16,128,128]{3,2,1,0:T(8,128)}, u32[]{:S(2)}) copy-start(f32[1,16,128,128]{3,2,1,0:T(8,128)} %reduce-scatter.2.cloned.1.call-done) | copy-start | bytes 3145732
  131.5 3.9 copy-start
  140.3 1.0 copy-start.2
  145.5 31.9 %all-to-all-start.4 = ((f32[1,16,128,128]{3,1,0,2:T(8,128)}), f32[1,16,128,128]{3,1,0,2:T(8,128)}, u32[]{:S(2)}, u32[]{:S(2)}) async-start(f32[1,16,128,128]{3,1,0,2:T(8,128)} %copy.182), calls=%async_computation.5 | async-start | bytes 2097152 | tf_op jit(solution)/shard_map/all_to_all | solution.py:61
  177.4 29.9 %all-to-all-start.5 = ((f32[1,16,128,128]{3,1,0,2:T(8,128)}), f32[1,16,128,128]{3,1,0,2:T(8,128)}, u32[]{:S(2)}, u32[]{:S(2)}) async-start(f32[1,16,128,128]{3,1,0,2:T(8,128)} %copy.187), calls=%async_computation.6 | async-start | bytes 2097152 | tf_op jit(solution)/shard_map/all_to_all | solution.py:62
  207.3 29.6 %all-to-all-start.1 = ((f32[1,16,128,128]{3,1,0,2:T(8,128)}), f32[1,16,128,128]{3,1,0,2:T(8,128)S(1)}, u32[]{:S(2)}, u32[]{:S(2)}) async-start(f32[1,16,128,128]{3,1,0,2:T(8,128)} %copy.161), calls=%async_computation.2 | async-start | bytes 2097152 | tf_op jit(solution)/shard_map/all_to_all | solution.py:62
  236.9 7.7 %copy-start.5 = (f32[1,16,128,128]{3,1,0,2:T(8,128)}, f32[1,16,128,128]{3,1,0,2:T(8,128)S(1)}, u32[]{:S(2)}) copy-start(f32[1,16,128,128]{3,1,0,2:T(8,128)S(1)} %all-to-all-done.1) | copy-start | bytes 3145732
  236.9 29.6 %all-to-all-start = ((f32[1,16,128,128]{3,1,0,2:T(8,128)}), f32[1,16,128,128]{3,1,0,2:T(8,128)S(1)}, u32[]{:S(2)}, u32[]{:S(2)}) async-start(f32[1,16,128,128]{3,1,0,2:T(8,128)} %copy.156), calls=%async_computation.1 | async-start | bytes 2097152 | tf_op jit(solution)/shard_map/all_to_all | solution.py:61
  266.5 1.0 copy-start.7
  267.4 30.1 %all-to-all-start.6 = ((f32[1,128,16,128]{3,2,0,1:T(8,128)}), f32[1,128,16,128]{3,2,0,1:T(8,128)S(1)}, u32[]{:S(2)}, u32[]{:S(2)}) async-start(f32[1,128,16,128]{3,2,0,1:T(8,128)} %copy.194), calls=%async_computation.7 | async-start | bytes 2097152 | tf_op jit(solution)/shard_map/all_to_all | solution.py:77
  272.8 28.9 %copy-start.6 = (f32[1,16,128,128]{3,1,0,2:T(8,128)S(1)}, f32[1,16,128,128]{3,1,0,2:T(8,128)}, u32[]{:S(2)}) copy-start(f32[1,16,128,128]{3,1,0,2:T(8,128)} %copy-done.5) | copy-start | bytes 3145732
  274.1 27.7 %copy-start.8 = (f32[1,16,128,128]{3,1,0,2:T(8,128)S(1)}, f32[1,16,128,128]{3,1,0,2:T(8,128)}, u32[]{:S(2)}) copy-start(f32[1,16,128,128]{3,1,0,2:T(8,128)} %copy-done.7) | copy-start | bytes 3145732
  297.5 29.9 %all-to-all-start.7 = ((f32[1,128,16,128]{3,2,0,1:T(8,128)}), f32[1,128,16,128]{3,2,0,1:T(8,128)}, u32[]{:S(2)}, u32[]{:S(2)}) async-start(f32[1,128,16,128]{3,2,0,1:T(8,128)} %copy.199), calls=%async_computation.8 | async-start | bytes 2097152 | tf_op jit(solution)/shard_map/all_to_all | solution.py:78
  327.4 29.8 %all-to-all-start.3 = ((f32[1,128,16,128]{3,2,0,1:T(8,128)}), f32[1,128,16,128]{3,2,0,1:T(8,128)}, u32[]{:S(2)}, u32[]{:S(2)}) async-start(f32[1,128,16,128]{3,2,0,1:T(8,128)} %copy.173), calls=%async_computation.4 | async-start | bytes 2097152 | tf_op jit(solution)/shard_map/all_to_all | solution.py:78
  357.2 29.7 %all-to-all-start.2 = ((f32[1,128,16,128]{3,2,0,1:T(8,128)}), f32[1,128,16,128]{3,2,0,1:T(8,128)}, u32[]{:S(2)}, u32[]{:S(2)}) async-start(f32[1,128,16,128]{3,2,0,1:T(8,128)} %copy.168), calls=%async_computation.3 | async-start | bytes 2097152 | tf_op jit(solution)/shard_map/all_to_all | solution.py:77
  362.8 4.0 copy-start.4
  394.9 3.7 copy-start.1
Sparse Core Ops, SparseCore 0:
  44.5 41.7 reduce-scatter.1
  88.5 34.4 all-gather.2
where the time goes:
time: 417 us; the launch traced here: 410 us
  waiting for transfers between devices  220 us (53%)
  matrix products  72.7 us (17%)
  starting transfers between devices  34.5 us (8%)
  blocking collectives  28.1 us (7%)
  local copies, waits for them, and re-layouts  23.3 us (6%)
  other arithmetic  16.7 us (4%)
  between operations  14.9 us (4%)
    reduce_scatter x1, waiting for transfers between devices, local(): lax.psum_scatter(jnp.einsum('bk,bxyz->kxyz', own_weights, orbitals, preci...  41.9 us
    all_to_all x2, waiting for transfers between devices, filtered(): lax.all_to_all(imag_part, 'grid', split_axis=2, concat_axis=1, tiled=True)  38.1 us
    all_to_all x2, waiting for transfers between devices, filtered(): lax.all_to_all(back_real, 'grid', split_axis=1, concat_axis=2, tiled=True)  36.9 us
    all_gather x1, waiting for transfers between devices, local(): lax.all_gather(localized, 'band', axis=0, tiled=True)  35.6 us
    all_to_all x2, waiting for transfers between devices, filtered(): lax.all_to_all(real_part, 'grid', split_axis=2, concat_axis=1, tiled=True)  34.3 us
    all_to_all x2, waiting for transfers between devices, filtered(): lax.all_to_all(back_imag, 'grid', split_axis=1, concat_axis=2, tiled=True)  33.2 us
    psum x1, blocking collectives, local(): own_rows = lax.psum(partial_pick, 'grid')  23.1 us
    all_to_all x2, starting transfers between devices, filtered(): lax.all_to_all(real_part, 'grid', split_axis=2, concat_axis=1, tiled=True)  9.39 us
  transfers between devices with their start and end apart: 10, of which 10 were waited for; matrix products, arithmetic and copies ran while one was open for 16% of the time, Pallas kernels for 0%

commit v1 on v0

v1 whole, which is shorter than its diff:
```python
import jax
import jax.numpy as jnp
from jax import lax
from jax.sharding import PartitionSpec as P

precise = lax.Precision.HIGHEST
swift = lax.Precision.HIGHEST


def tables(length):
    across = jnp.arange(length, dtype=jnp.int32)
    phases = across[:, None] * across[None, :] % length
    angles = phases.astype(jnp.float32) * (2.0 * jnp.pi / length)
    return (jnp.cos(angles), jnp.sin(angles))


def wrapped(indices, length):
    return jnp.where(indices < length // 2, indices, indices - length)


def coulomb(length, plane_start, plane_count):
    wave_first = wrapped(jnp.arange(length, dtype=jnp.int32), length).astype(jnp.float32)
    wave_second = wrapped(plane_start + jnp.arange(plane_count, dtype=jnp.int32), length).astype(
        jnp.float32
    )
    squared = (
        wave_first[:, None, None] ** 2
        + wave_second[None, :, None] ** 2
        + wave_first[None, None, :] ** 2
    )
    scaling = float(length) ** 1.5
    return jnp.where(squared > 0, 0.25 / (scaling * jnp.maximum(squared, 1.0)), 0.0)


def filtered(real_in, imag_in, kernel, cos_table, sin_table):
    real_part = jnp.dot(real_in, cos_table, precision=swift) + jnp.dot(
        imag_in, sin_table, precision=swift
    )
    imag_part = jnp.dot(imag_in, cos_table, precision=swift) - jnp.dot(
        real_in, sin_table, precision=swift
    )
    real_part, imag_part = (
        jnp.einsum("pxyz,yk->pxkz", real_part, cos_table, precision=swift)
        + jnp.einsum("pxyz,yk->pxkz", imag_part, sin_table, precision=swift),
        jnp.einsum("pxyz,yk->pxkz", imag_part, cos_table, precision=swift)
        - jnp.einsum("pxyz,yk->pxkz", real_part, sin_table, precision=swift),
    )
    real_wide = lax.all_to_all(real_part, "grid", split_axis=2, concat_axis=1, tiled=True)
    imag_wide = lax.all_to_all(imag_part, "grid", split_axis=2, concat_axis=1, tiled=True)
    ahead_real = (
        jnp.einsum("pxyz,xk->pkyz", real_wide, cos_table, precision=swift)
        + jnp.einsum("pxyz,xk->pkyz", imag_wide, sin_table, precision=swift)
    ) * kernel
    ahead_imag = (
        jnp.einsum("pxyz,xk->pkyz", imag_wide, cos_table, precision=swift)
        - jnp.einsum("pxyz,xk->pkyz", real_wide, sin_table, precision=swift)
    ) * kernel
    back_real = jnp.einsum("pxyz,xk->pkyz", ahead_real, cos_table, precision=swift) - jnp.einsum(
        "pxyz,xk->pkyz", ahead_imag, sin_table, precision=swift
    )
    back_imag = jnp.einsum("pxyz,xk->pkyz", ahead_imag, cos_table, precision=swift) + jnp.einsum(
        "pxyz,xk->pkyz", ahead_real, sin_table, precision=swift
    )
    real_part = lax.all_to_all(back_real, "grid", split_axis=1, concat_axis=2, tiled=True)
    imag_part = lax.all_to_all(back_imag, "grid", split_axis=1, concat_axis=2, tiled=True)
    real_part, imag_part = (
        jnp.einsum("pxyz,yk->pxkz", real_part, cos_table, precision=swift)
        - jnp.einsum("pxyz,yk->pxkz", imag_part, sin_table, precision=swift),
        jnp.einsum("pxyz,yk->pxkz", imag_part, cos_table, precision=swift)
        + jnp.einsum("pxyz,yk->pxkz", real_part, sin_table, precision=swift),
    )
    out_real = jnp.dot(real_part, cos_table, precision=swift) - jnp.dot(
        imag_part, sin_table, precision=swift
    )
    out_imag = jnp.dot(imag_part, cos_table, precision=swift) + jnp.dot(
        real_part, sin_table, precision=swift
    )
    return (out_real, out_imag)


def assignment(pattern):
    blocks = pattern.shape[0]
    ids = jnp.arange(blocks, dtype=jnp.int32)
    off = ((pattern == 1) & (ids[:, None] != ids[None, :])).astype(jnp.int32).reshape(-1)
    before = jnp.cumsum(off) - off
    chosen = (off[None, :] == 1) & (before[None, :] == ids[:, None])
    chosen = chosen.reshape(blocks, blocks, blocks)
    firsts = jnp.any(chosen, axis=2).astype(jnp.float32)
    seconds = jnp.any(chosen, axis=1).astype(jnp.float32)
    return firsts, seconds


def mixed(coefficients, bands):
    total = coefficients[0] * bands[0]
    for band in range(1, bands.shape[0]):
        total = total + coefficients[band] * bands[band]
    return total


def local(orbitals, pivots, pattern):
    slab_planes = orbitals.shape[1]
    length = orbitals.shape[3]
    block_total = pattern.shape[0]
    grid_index = lax.axis_index("grid")
    band_index = lax.axis_index("band")
    every = lax.all_gather(orbitals, "band", axis=0, tiled=True)
    local_cell = pivots - grid_index * (slab_planes * length * length)
    inside = (local_cell >= 0) & (local_cell < slab_planes * length * length)
    cell = jnp.clip(local_cell, 0, slab_planes * length * length - 1)
    rows = jnp.take(orbitals.reshape(slab_planes * length, length), cell // length, axis=0)
    lanes = jnp.arange(length, dtype=jnp.int32)
    sampled = jnp.sum(jnp.where(lanes[None, :] == (cell % length)[:, None], rows, 0.0), axis=1)
    own = jnp.where(inside, sampled, 0.0)
    ids = jnp.arange(block_total, dtype=jnp.int32)
    picked = lax.psum(
        jnp.where(ids[:, None] == band_index, own[None, :], 0.0), ("band", "grid")
    )
    gram_matrix = jnp.dot(picked.T, picked, precision=precise)
    factor = jnp.linalg.cholesky(gram_matrix)
    rotation = lax.linalg.triangular_solve(factor, picked.T, left_side=True, lower=True).T
    firsts, seconds = assignment(pattern)
    selectors = jnp.stack(
        [
            (ids == band_index).astype(jnp.float32),
            lax.dynamic_index_in_dim(firsts, band_index, 0, keepdims=False),
            lax.dynamic_index_in_dim(seconds, band_index, 0, keepdims=False),
        ]
    )
    coefficients = jnp.dot(selectors, rotation.T, precision=precise)
    localized = mixed(coefficients[0], every)
    first = mixed(coefficients[1], every)
    second = mixed(coefficients[2], every)
    cos_table, sin_table = tables(length)
    plane_count = length // lax.axis_size("grid")
    kernel = coulomb(length, grid_index * plane_count, plane_count)
    potential_own, potential_off = filtered(
        (localized * localized)[None], (first * second)[None], kernel, cos_table, sin_table
    )
    terms = lax.all_gather(potential_off[0] * second, "band", axis=0, tiled=False)
    weights = lax.dynamic_index_in_dim(firsts, band_index, 1, keepdims=False)
    exchange_term = potential_own[0] * localized + mixed(weights, terms)
    return (localized[None], exchange_term[None])


def solution(mesh):
    return jax.shard_map(
        local,
        mesh=mesh,
        in_specs=(P("band", "grid", None, None), P(), P()),
        out_specs=(P("band", "grid", None, None), P("band", "grid", None, None)),
        check_vma=False,
    )
```

time: 417 us -> 279 us (0.67)
  waiting for transfers between devices: 220 us -> 121 us
  matrix products: 72.7 us -> 39.3 us
  blocking collectives: 28.1 us -> 42 us
  local copies, waits for them, and re-layouts: 23.3 us -> 13.3 us
  starting transfers between devices: 34.5 us -> 27.1 us
    reduce_scatter x1 -> x0, waiting for transfers between devices: 41.9 us -> none  [local(): lax.psum_scatter(jnp.einsum('bk,bxyz->kxyz', own_weights, orbitals, preci...]
    dot_general x49 -> x25, matrix products: 72.4 us -> 38.9 us  [the longest x1 7.33 us: filtered(): jnp.dot(imag_part, sin_table, precision=swift)]
    psum x1, blocking collectives: 23.1 us -> 42 us  [local(): lax.psum(jnp.where(ids[:, None] == band_index, own[None, :], 0.0), ('band...]
    all_to_all x2 -> x1, waiting for transfers between devices: 38.1 us -> 20.1 us  [filtered(): lax.all_to_all(imag_part, 'grid', split_axis=2, concat_axis=1, tiled=True)]
    all_to_all x2 -> x1, waiting for transfers between devices: 36.9 us -> 24.2 us  [filtered(): lax.all_to_all(back_real, 'grid', split_axis=1, concat_axis=2, tiled=True)]
    all_to_all x2 -> x1, waiting for transfers between devices: 33.2 us -> 20.5 us  [filtered(): lax.all_to_all(back_imag, 'grid', split_axis=1, concat_axis=2, tiled=True)]
    all_to_all x2 -> x1, waiting for transfers between devices: 34.3 us -> 24.2 us  [filtered(): lax.all_to_all(real_part, 'grid', split_axis=2, concat_axis=1, tiled=True)]
    all_to_all x2 -> x1, starting transfers between devices: 9.39 us -> 3.56 us  [filtered(): lax.all_to_all(real_part, 'grid', split_axis=2, concat_axis=1, tiled=True)]
  transfers between devices with their start and end apart: 10 -> 6, of which waited for: 10 -> 5; matrix products, arithmetic and copies ran while one was open for 16% -> 9% of each run, Pallas kernels for 0% -> 0%
where the time goes in v1:
time: 279 us; the launch traced here: 276 us
  waiting for transfers between devices  121 us (43%)
  blocking collectives  42 us (15%)
  matrix products  39.3 us (14%)
  starting transfers between devices  27.1 us (10%)
  other arithmetic  17.9 us (6%)
  between operations  14.6 us (5%)
  local copies, waits for them, and re-layouts  13.3 us (5%)
    psum x1, blocking collectives, local(): lax.psum(jnp.where(ids[:, None] == band_index, own[None, :], 0.0), ('band...  42 us
    all_gather x1, waiting for transfers between devices, local(): lax.all_gather(potential_off[0] * second, 'band', axis=0, tiled=False)  31.7 us
    all_to_all x1, waiting for transfers between devices, filtered(): lax.all_to_all(real_part, 'grid', split_axis=2, concat_axis=1, tiled=True)  24.2 us
    all_to_all x1, waiting for transfers between devices, filtered(): lax.all_to_all(back_real, 'grid', split_axis=1, concat_axis=2, tiled=True)  24.2 us
    all_to_all x1, waiting for transfers between devices, filtered(): lax.all_to_all(back_imag, 'grid', split_axis=1, concat_axis=2, tiled=True)  20.5 us
    all_to_all x1, waiting for transfers between devices, filtered(): lax.all_to_all(imag_part, 'grid', split_axis=2, concat_axis=1, tiled=True)  20.1 us
    all_to_all x1, starting transfers between devices, filtered(): lax.all_to_all(back_imag, 'grid', split_axis=1, concat_axis=2, tiled=True)  14.2 us
    mul x1, other arithmetic, local(): first * second  8.99 us
  transfers between devices with their start and end apart: 6, of which 5 were waited for; matrix products, arithmetic and copies ran while one was open for 9% of the time, Pallas kernels for 0%

profile of v1, /device:TPU:0, one launch (start us, length us, event | category | flops | bytes accessed | tf_op | source)
XLA Modules:
  0.0 275.6 jit_solution(101690971523328140)
XLA Ops:
  8.6 1.8 gather_fusion
  11.3 42.0 %psum.7 = f32[4,4]{1,0:T(4,128)S(1)} all-reduce(f32[4,4]{1,0:T(4,128)S(1)} %broadcast_select_fusion), channel_id=1, replica_groups=mesh['band'=4,'grid'=8] {'band','grid'}, use_global_device_ids=true, to_apply=%region_4.5 | all-reduce | flops 16 | bytes 128 | tf_op jit(solution)/shard_map/psum | solution.py:115
  59.8 9.0 %add_multiply_fusion = (f32[1,16,128,128]{3,2,1,0:T(8,128)S(1)}, f32[1,16,128,128]{3,2,1,0:T(8,128)}) fusion(f32[4,16,128,128]{3,2,1,0:T(8,128)} %all-gather.3.cloned.1.call-done, f32[]{:T(128)} %bitcast.17, f32[]{:T(128)} %bitcast.16, f32[]{:T(128)} %bitcast.15, f32[]{:T(128)} %bitcast.14, f32[]{:T(128)} %bitcast.21, f32[]{:T(128)} %bitcast.20, ...), kind=kLoop, calls=%fused_computation.45 | loop fusion | flops 3932160 | bytes 6291488 | tf_op jit(solution)/shard_map/mul | solution.py:137
  70.1 2.8 %multiply_add_fusion.1 = f32[1,16,128,128]{3,2,1,0:T(8,128)S(1)} fusion(f32[4,16,128,128]{3,2,1,0:T(8,128)S(1)} %copy-done.1, f32[]{:T(128)} %bitcast.7, f32[]{:T(128)} %bitcast.6, f32[]{:T(128)} %bitcast.5, f32[]{:T(128)} %bitcast.4), kind=kLoop, calls=%fused_computation.46 | loop fusion | flops 1835008 | bytes 5242896 | tf_op jit(solution)/shard_map/add | solution.py:96
  79.2 1.6 copy.62
  80.8 5.7 %all-to-all-start.1 = ((f32[1,16,128,128]{3,1,0,2:T(8,128)}), f32[1,16,128,128]{3,1,0,2:T(8,128)}, u32[]{:S(2)}, u32[]{:S(2)}) async-start(f32[1,16,128,128]{3,1,0,2:T(8,128)} %copy.62), calls=%async_computation.1 | async-start | bytes 2097152 | tf_op jit(solution)/shard_map/all_to_all | solution.py:49
  89.1 1.6 copy.57
  90.7 20.1 %all-to-all-done.1 = f32[1,16,128,128]{3,1,0,2:T(8,128)} async-done(((f32[1,16,128,128]{3,1,0,2:T(8,128)}), f32[1,16,128,128]{3,1,0,2:T(8,128)}, u32[]{:S(2)}, u32[]{:S(2)}) %all-to-all-start.1) | async-done | bytes 1048608 | tf_op jit(solution)/shard_map/all_to_all | solution.py:49
  110.8 3.6 %all-to-all-start = ((f32[1,16,128,128]{3,1,0,2:T(8,128)}), f32[1,16,128,128]{3,1,0,2:T(8,128)S(1)}, u32[]{:S(2)}, u32[]{:S(2)}) async-start(f32[1,16,128,128]{3,1,0,2:T(8,128)} %copy.57), calls=%async_computation | async-start | bytes 2097152 | tf_op jit(solution)/shard_map/all_to_all | solution.py:48
  114.5 1.3 copy.63
  115.8 24.2 %all-to-all-done = f32[1,16,128,128]{3,1,0,2:T(8,128)S(1)} async-done(((f32[1,16,128,128]{3,1,0,2:T(8,128)}), f32[1,16,128,128]{3,1,0,2:T(8,128)S(1)}, u32[]{:S(2)}, u32[]{:S(2)}) %all-to-all-start) | async-done | bytes 1048608 | tf_op jit(solution)/shard_map/all_to_all | solution.py:48
  142.7 1.5 fusion.7
  144.2 1.5 fusion.6
  148.2 1.6 copy.74
  149.9 14.2 %all-to-all-start.3 = ((f32[1,128,16,128]{3,2,0,1:T(8,128)}), f32[1,128,16,128]{3,2,0,1:T(8,128)}, u32[]{:S(2)}, u32[]{:S(2)}) async-start(f32[1,128,16,128]{3,2,0,1:T(8,128)} %copy.74), calls=%async_computation.3 | async-start | bytes 2097152 | tf_op jit(solution)/shard_map/all_to_all | solution.py:65
  166.6 1.6 copy.69
  168.2 20.5 %all-to-all-done.3 = f32[1,128,16,128]{3,2,0,1:T(8,128)} async-done(((f32[1,128,16,128]{3,2,0,1:T(8,128)}), f32[1,128,16,128]{3,2,0,1:T(8,128)}, u32[]{:S(2)}, u32[]{:S(2)}) %all-to-all-start.3) | async-done | bytes 1048608 | tf_op jit(solution)/shard_map/all_to_all | solution.py:65
  188.8 3.6 %all-to-all-start.2 = ((f32[1,128,16,128]{3,2,0,1:T(8,128)}), f32[1,128,16,128]{3,2,0,1:T(8,128)S(1)}, u32[]{:S(2)}, u32[]{:S(2)}) async-start(f32[1,128,16,128]{3,2,0,1:T(8,128)} %copy.69), calls=%async_computation.2 | async-start | bytes 2097152 | tf_op jit(solution)/shard_map/all_to_all | solution.py:64
  192.4 1.3 copy.75
  193.7 24.2 %all-to-all-done.2 = f32[1,128,16,128]{3,2,0,1:T(8,128)S(1)} async-done(((f32[1,128,16,128]{3,2,0,1:T(8,128)}), f32[1,128,16,128]{3,2,0,1:T(8,128)S(1)}, u32[]{:S(2)}, u32[]{:S(2)}) %all-to-all-start.2) | async-done | bytes 1048608 | tf_op jit(solution)/shard_map/all_to_all | solution.py:64
  224.4 2.2 fusion.12
  227.3 2.2 fusion.52
  229.5 31.7 %all-gather.5.cloned.1.call-done = f32[4,16,128,128]{3,2,1,0:T(8,128)} async-done(((f32[1,16,128,128]{3,2,1,0:T(8,128)}), f32[4,16,128,128]{3,2,1,0:T(8,128)}) %all-gather.5.cloned.1.call-update) | async-done | bytes 4194320 | tf_op jit(solution)/shard_map/all_gather | solution.py:139
  261.2 7.3 %fusion.11 = f32[1,16,128,128]{3,2,1,0:T(8,128)} fusion(f32[1,16,128,128]{3,2,1,0:T(8,128)S(1)} %multiply_add_fusion.1, f32[16,128,128]{2,1,0:T(8,128)} %fusion.52, f32[16,128,128]{2,1,0:T(8,128)S(1)} %fusion.2, f32[4,16,128,128]{3,2,1,0:T(8,128)} %all-gather.5.cloned.1.call-done, f32[]{:T(128)} %bitcast.73, f32[]{:T(128)} %bitcast.72, f32[]{:T(128)} %bitcast.71, ...), kind=kOutput, calls=%fused_computation.26 | convolution fusion | flops 405504000 | bytes 8388624 | tf_op jit(solution)/shard_map/dot_general | solution.py:72
  (67 shorter events, 34.0 us)
Async XLA Ops:
  7.2 52.7 %all-gather.3.cloned.1.call-start = ((), (), s32[]{:S(2)}) async-start(), calls=%async_computation.4 | async-start | bytes 5242880 | tf_op jit(solution)/shard_map/all_gather | solution.py:106
  59.8 10.2 %copy-start.1 = (f32[4,16,128,128]{3,2,1,0:T(8,128)S(1)}, f32[4,16,128,128]{3,2,1,0:T(8,128)}, u32[]{:S(2)}) copy-start(f32[4,16,128,128]{3,2,1,0:T(8,128)} %all-gather.3.cloned.1.call-done) | copy-start | bytes 12582916
  72.8 188.4 %copy-start = (f32[1,16,128,128]{3,2,1,0:T(8,128)}, f32[1,16,128,128]{3,2,1,0:T(8,128)S(1)}, u32[]{:S(2)}) copy-start(f32[1,16,128,128]{3,2,1,0:T(8,128)S(1)} %multiply_add_fusion.1) | copy-start | bytes 3145732
  80.8 30.0 %all-to-all-start.1 = ((f32[1,16,128,128]{3,1,0,2:T(8,128)}), f32[1,16,128,128]{3,1,0,2:T(8,128)}, u32[]{:S(2)}, u32[]{:S(2)}) async-start(f32[1,16,128,128]{3,1,0,2:T(8,128)} %copy.62), calls=%async_computation.1 | async-start | bytes 2097152 | tf_op jit(solution)/shard_map/all_to_all | solution.py:49
  110.8 29.2 %all-to-all-start = ((f32[1,16,128,128]{3,1,0,2:T(8,128)}), f32[1,16,128,128]{3,1,0,2:T(8,128)S(1)}, u32[]{:S(2)}, u32[]{:S(2)}) async-start(f32[1,16,128,128]{3,1,0,2:T(8,128)} %copy.57), calls=%async_computation | async-start | bytes 2097152 | tf_op jit(solution)/shard_map/all_to_all | solution.py:48
  149.9 38.9 %all-to-all-start.3 = ((f32[1,128,16,128]{3,2,0,1:T(8,128)}), f32[1,128,16,128]{3,2,0,1:T(8,128)}, u32[]{:S(2)}, u32[]{:S(2)}) async-start(f32[1,128,16,128]{3,2,0,1:T(8,128)} %copy.74), calls=%async_computation.3 | async-start | bytes 2097152 | tf_op jit(solution)/shard_map/all_to_all | solution.py:65
  188.8 29.1 %all-to-all-start.2 = ((f32[1,128,16,128]{3,2,0,1:T(8,128)}), f32[1,128,16,128]{3,2,0,1:T(8,128)S(1)}, u32[]{:S(2)}, u32[]{:S(2)}) async-start(f32[1,128,16,128]{3,2,0,1:T(8,128)} %copy.69), calls=%async_computation.2 | async-start | bytes 2097152 | tf_op jit(solution)/shard_map/all_to_all | solution.py:64
  192.3 68.9 %all-gather.5.cloned.1.call-start = ((), (), s32[]{:S(2)}) async-start(), calls=%async_computation.5 | async-start | bytes 5242880 | tf_op jit(solution)/shard_map/all_gather | solution.py:139
  220.6 3.8 %copy-start.2 = (f32[1,16,128,128]{3,2,1,0:T(8,128)S(1)}, f32[1,16,128,128]{3,2,1,0:T(8,128)}, u32[]{:S(2)}) copy-start(f32[1,16,128,128]{3,2,1,0:T(8,128)} %get-tuple-element.5) | copy-start | bytes 3145732
Sparse Core Ops, SparseCore 0:
  9.6 37.4 all-gather.2
  226.8 34.3 all-gather.4

commit v2 on v1

v2 whole, which is shorter than its diff:
```python
import functools

import jax
import jax.numpy as jnp
import numpy as np
from jax import lax
from jax.experimental import pallas as pl
from jax.experimental.pallas import tpu as pltpu
from jax.sharding import PartitionSpec as P

precise = lax.Precision.HIGHEST
MESH = pl.DeviceIdType.MESH


def complex_table(length):
    across = np.arange(length)
    angles = (across[:, None] * across[None, :] % length) * (2.0 * np.pi / length)
    cosine, sine = np.cos(angles), np.sin(angles)
    return np.block([[cosine, -sine], [sine, cosine]]).astype(np.float32)


def wrapped(indices, length):
    return jnp.where(indices < length // 2, indices, indices - length)


def coulomb(length, row_start, row_count):
    wave = wrapped(jnp.arange(length, dtype=jnp.int32), length).astype(jnp.float32)
    rows = wrapped(row_start + jnp.arange(row_count, dtype=jnp.int32), length).astype(jnp.float32)
    squared = rows[:, None, None] ** 2 + wave[None, :, None] ** 2 + wave[None, None, :] ** 2
    scaling = float(length) ** 1.5
    return jnp.where(squared > 0, 0.25 / (scaling * jnp.maximum(squared, 1.0)), 0.0)


def times(left, right):
    return jnp.dot(left, right, precision=precise, preferred_element_type=jnp.float32)


def transform_kernel(
    n, halves, chunks,
    own_ref, first_ref, second_ref, kern_ref, fwd_ref, bwd_ref,
    term_ref, off_ref,
    send_one, recv_one, send_two, recv_two,
    sems_one_send, sems_one_recv, sems_two_send, sems_two_recv, sems_own,
):
    planes, length = own_ref.shape[0], own_ref.shape[2]
    depth = length // n
    rows = depth // halves
    chunk = planes // chunks
    me = lax.axis_index("grid")
    barrier = pltpu.get_barrier_semaphore()
    for step in range(1, n):
        pl.semaphore_signal(
            barrier, inc=1, device_id={"grid": lax.rem(me + step, n)}, device_id_type=MESH
        )
    pl.semaphore_wait(barrier, n - 1)

    def out_copies(part, half):
        size = chunk * rows
        mine = pl.ds(pl.multiple_of(me * (planes * rows) + part * size, size), size)
        copies = []
        for step in range(1, n):
            target = lax.rem(me + step, n)
            copies.append(
                pltpu.make_async_remote_copy(
                    src_ref=send_one.at[target, half, :, pl.ds(part * size, size), :],
                    dst_ref=recv_one.at[half, :, mine, :],
                    send_sem=sems_one_send.at[part, half, step],
                    recv_sem=sems_one_recv.at[part, half, step],
                    device_id={"grid": target},
                    device_id_type=MESH,
                )
            )
        return copies

    def own_copy(half):
        size = planes * rows
        return pltpu.make_async_copy(
            send_one.at[me, half],
            recv_one.at[half, :, pl.ds(pl.multiple_of(me * size, size), size), :],
            sems_own.at[half],
        )

    def back_copies(half):
        size = planes * rows
        copies = []
        for step in range(1, n):
            target = lax.rem(me + step, n)
            copies.append(
                pltpu.make_async_remote_copy(
                    src_ref=send_two.at[half, :, pl.ds(pl.multiple_of(target * size, size), size), :],
                    dst_ref=recv_two.at[half, me],
                    send_sem=sems_two_send.at[half, step],
                    recv_sem=sems_two_recv.at[half, step],
                    device_id={"grid": target},
                    device_id_type=MESH,
                )
            )
        return copies

    def own_back(half):
        size = planes * rows
        return pltpu.make_async_copy(
            send_two.at[half, :, pl.ds(pl.multiple_of(me * size, size), size), :],
            recv_two.at[half, me],
            sems_own.at[halves + half],
        )

    def ahead(pair, carry):
        pieces = []
        for which in range(2):
            plane = pair * 2 + which
            own = own_ref[plane]
            both = jnp.concatenate([own * own, first_ref[plane] * second_ref[plane]], axis=1)
            spectrum = times(both, fwd_ref[...])
            pieces.append(
                jnp.concatenate([spectrum[:, :length], spectrum[:, length:]], axis=0)
            )
        result = times(bwd_ref[...], jnp.concatenate(pieces, axis=1))
        for which in range(2):
            for target in range(n):
                for half in range(halves):
                    for part in range(2):
                        low = part * length + target * depth + half * rows
                        send_one[target, half, part, pl.ds((pair * 2 + which) * rows, rows), :] = (
                            result[low : low + rows, which * length : (which + 1) * length]
                        )
        return carry

    for part in range(chunks):
        lax.fori_loop(part * chunk // 2, (part + 1) * chunk // 2, ahead, 0)
        for copy in out_copies(part, 0):
            copy.start()
    for half in range(1, halves):
        for part in range(chunks):
            for copy in out_copies(part, half):
                copy.start()
    for half in range(halves):
        own_copy(half).start()

    for half in range(halves):
        own_copy(half).wait()
        for part in range(chunks):
            for copy in out_copies(part, half):
                copy.wait_recv()

        def columns(pair, carry):
            pieces = []
            for which in range(2):
                place = pl.ds(pair * 2 + which, length, stride=rows)
                pieces.append(
                    jnp.concatenate(
                        [recv_one[half, 0, place, :], recv_one[half, 1, place, :]], axis=0
                    )
                )
            spectrum = times(bwd_ref[...], jnp.concatenate(pieces, axis=1))
            weights = jnp.concatenate(
                [kern_ref[half * rows + pair * 2], kern_ref[half * rows + pair * 2 + 1]], axis=1
            )
            spectrum = spectrum * jnp.concatenate([weights, weights], axis=0)
            result = times(fwd_ref[...], spectrum)
            for which in range(2):
                place = pl.ds(pair * 2 + which, length, stride=rows)
                lanes = slice(which * length, (which + 1) * length)
                send_two[half, 0, place, :] = result[:length, lanes]
                send_two[half, 1, place, :] = result[length:, lanes]
            return carry

        lax.fori_loop(0, rows // 2, columns, 0)
        for copy in back_copies(half):
            copy.start()
        own_back(half).start()

    for half in range(halves):
        own_back(half).wait()
        for copy in back_copies(half):
            copy.wait_recv()

    def home(pair, carry):
        pieces = []
        for which in range(2):
            place = pl.ds((pair * 2 + which) * rows, rows)
            pieces.append(
                jnp.concatenate(
                    [
                        recv_two[half, source, part, place, :]
                        for part in range(2)
                        for source in range(n)
                        for half in range(halves)
                    ],
                    axis=0,
                )
            )
        result = times(fwd_ref[...], jnp.concatenate(pieces, axis=1))
        for which in range(2):
            plane = pair * 2 + which
            lanes = slice(which * length, (which + 1) * length)
            both = jnp.concatenate([result[:length, lanes], result[length:, lanes]], axis=1)
            potential = times(both, bwd_ref[...])
            term_ref[plane] = potential[:, :length] * own_ref[plane]
            off_ref[plane] = potential[:, length:] * second_ref[plane]
        return carry

    lax.fori_loop(0, planes // 2, home, 0)
    for half in range(halves):
        for part in range(chunks):
            for copy in out_copies(part, half):
                copy.wait_send()
        for copy in back_copies(half):
            copy.wait_send()


def terms_of(own, first, second, kernel):
    n = lax.axis_size("grid")
    planes, length = own.shape[0], own.shape[2]
    depth = length // n
    halves = 2 if depth % 16 == 0 else 1
    rows = depth // halves
    chunk = max(planes // 4, 2)
    chunks = planes // chunk
    forward = complex_table(length)
    vmem = pl.BlockSpec(memory_space=pltpu.VMEM)
    slab = jax.ShapeDtypeStruct(own.shape, jnp.float32)
    block = planes * rows
    return pl.pallas_call(
        functools.partial(transform_kernel, n, halves, chunks),
        out_shape=(slab, slab),
        in_specs=[vmem] * 6,
        out_specs=(vmem, vmem),
        scratch_shapes=[
            pltpu.VMEM((n, halves, 2, block, length), jnp.float32),
            pltpu.VMEM((halves, 2, n * block, length), jnp.float32),
            pltpu.VMEM((halves, 2, n * block, length), jnp.float32),
            pltpu.VMEM((halves, n, 2, block, length), jnp.float32),
            pltpu.SemaphoreType.DMA((chunks, halves, n)),
            pltpu.SemaphoreType.DMA((chunks, halves, n)),
            pltpu.SemaphoreType.DMA((halves, n)),
            pltpu.SemaphoreType.DMA((halves, n)),
            pltpu.SemaphoreType.DMA((2 * halves,)),
        ],
        compiler_params=pltpu.CompilerParams(
            collective_id=0, has_side_effects=True, vmem_limit_bytes=40 * 1024 * 1024
        ),
    )(own, first, second, kernel, jnp.asarray(forward), jnp.asarray(forward.T.copy()))


def assignment(pattern):
    blocks = pattern.shape[0]
    ids = jnp.arange(blocks, dtype=jnp.int32)
    off = ((pattern == 1) & (ids[:, None] != ids[None, :])).astype(jnp.int32).reshape(-1)
    before = jnp.cumsum(off) - off
    chosen = (off[None, :] == 1) & (before[None, :] == ids[:, None])
    chosen = chosen.reshape(blocks, blocks, blocks)
    firsts = jnp.any(chosen, axis=2).astype(jnp.float32)
    seconds = jnp.any(chosen, axis=1).astype(jnp.float32)
    return firsts, seconds


def mixed(coefficients, bands):
    total = coefficients[0] * bands[0]
    for band in range(1, bands.shape[0]):
        total = total + coefficients[band] * bands[band]
    return total


def local(orbitals, pivots, pattern):
    slab_planes = orbitals.shape[1]
    length = orbitals.shape[3]
    block_total = pattern.shape[0]
    grid_index = lax.axis_index("grid")
    band_index = lax.axis_index("band")
    every = lax.all_gather(orbitals, "band", axis=0, tiled=True)
    local_cell = pivots - grid_index * (slab_planes * length * length)
    inside = (local_cell >= 0) & (local_cell < slab_planes * length * length)
    cell = jnp.clip(local_cell, 0, slab_planes * length * length - 1)
    rows = jnp.take(orbitals.reshape(slab_planes * length, length), cell // length, axis=0)
    lanes = jnp.arange(length, dtype=jnp.int32)
    sampled = jnp.sum(jnp.where(lanes[None, :] == (cell % length)[:, None], rows, 0.0), axis=1)
    own = jnp.where(inside, sampled, 0.0)
    ids = jnp.arange(block_total, dtype=jnp.int32)
    picked = lax.psum(
        jnp.where(ids[:, None] == band_index, own[None, :], 0.0), ("band", "grid")
    )
    gram_matrix = jnp.dot(picked.T, picked, precision=precise)
    factor = jnp.linalg.cholesky(gram_matrix)
    rotation = lax.linalg.triangular_solve(factor, picked.T, left_side=True, lower=True).T
    firsts, seconds = assignment(pattern)
    selectors = jnp.stack(
        [
            (ids == band_index).astype(jnp.float32),
            lax.dynamic_index_in_dim(firsts, band_index, 0, keepdims=False),
            lax.dynamic_index_in_dim(seconds, band_index, 0, keepdims=False),
        ]
    )
    coefficients = jnp.dot(selectors, rotation.T, precision=precise)
    localized = mixed(coefficients[0], every)
    first = mixed(coefficients[1], every)
    second = mixed(coefficients[2], every)
    depth = length // lax.axis_size("grid")
    kernel = coulomb(length, grid_index * depth, depth)
    own_term, off_term = terms_of(localized, first, second, kernel)
    terms = lax.all_gather(off_term, "band", axis=0, tiled=False)
    weights = lax.dynamic_index_in_dim(firsts, band_index, 1, keepdims=False)
    exchange_term = own_term + mixed(weights, terms)
    return (localized[None], exchange_term[None])


def solution(mesh):
    return jax.shard_map(
        local,
        mesh=mesh,
        in_specs=(P("band", "grid", None, None), P(), P()),
        out_specs=(P("band", "grid", None, None), P("band", "grid", None, None)),
        check_vma=False,
    )
```

time: 279 us -> 226 us (0.81); the launches traced: 276 us -> 225 us
  Pallas kernels: 0 us -> 99.3 us
  waiting for transfers between devices: 121 us -> 35.6 us
  matrix products: 39.3 us -> 0.53 us
  starting transfers between devices: 27.1 us -> 0.08 us
  other arithmetic: 17.9 us -> 29.7 us
  local copies, waits for them, and re-layouts: 13.3 us -> 3.97 us
    pallas_call x0 -> x1, Pallas kernels: none -> 99.3 us  [terms_of(): pl.pallas_call(functools.partial(transform_kernel, n, halves, chunks), ou...]
    all_to_all x4 -> x0, waiting for transfers between devices: 89 us -> none  [the longest x1 24.2 us: filtered(): lax.all_to_all(real_part, 'grid', split_axis=2, concat_axis=1, tiled=True)]
    dot_general x24 -> x0, matrix products: 38.8 us -> none  [the longest x1 7.33 us: filtered(): jnp.dot(imag_part, sin_table, precision=swift)]
    all_to_all x4 -> x0, starting transfers between devices: 27 us -> none  [the longest x1 14.2 us: filtered(): lax.all_to_all(back_imag, 'grid', split_axis=1, concat_axis=2, tiled=True)]
    add x1 -> x3, other arithmetic: 2.76 us -> 17.2 us  [mixed(): total = total + coefficients[band] * bands[band]]
    mul x1 -> x0, other arithmetic: 8.99 us -> none  [local(): first * second]
    broadcast_in_dim x0 -> x1, other arithmetic: none -> 6.1 us  [local(): return (localized[None], exchange_term[None])]
    sub x2 -> x0, local copies, waits for them, and re-layouts: 3.25 us -> none  [the longest x1 1.64 us: filtered(): jnp.einsum('pxyz,xk->pkyz', ahead_real, cos_table, precision=swift)]
  transfers between devices with their start and end apart: 6 -> 2, of which waited for: 5 -> 1; matrix products, arithmetic and copies ran while one was open for 9% -> 8% of each run, Pallas kernels for 0% -> 0%
where the time goes in v2:
time: 226 us; the launch traced here: 225 us
  Pallas kernels  99.3 us (44%)
  blocking collectives  42 us (19%)
  waiting for transfers between devices  35.6 us (16%)
  other arithmetic  29.7 us (13%)
  between operations  14.2 us (6%)
  local copies, waits for them, and re-layouts  3.97 us (2%)
    pallas_call x1, Pallas kernels, terms_of(): pl.pallas_call(functools.partial(transform_kernel, n, halves, chunks), ou...  99.3 us
    psum x1, blocking collectives, local(): lax.psum(jnp.where(ids[:, None] == band_index, own[None, :], 0.0), ('band...  42 us
    all_gather x1, waiting for transfers between devices, local(): terms = lax.all_gather(off_term, 'band', axis=0, tiled=False)  34.8 us
    add x3, other arithmetic, mixed(): total = total + coefficients[band] * bands[band]  17.2 us
    broadcast_in_dim x1, other arithmetic, local(): return (localized[None], exchange_term[None])  6.1 us
  transfers between devices with their start and end apart: 2, of which 1 were waited for; matrix products, arithmetic and copies ran while one was open for 8% of the time, Pallas kernels for 0%

profile of v2, /device:TPU:0, one launch (start us, length us, event | category | flops | bytes accessed | tf_op | source)
XLA Modules:
  0.0 225.5 jit_solution(5914590445492860761)
XLA Ops:
  7.2 0.7 all-gather.4.cloned.1.call-update
  7.9 0.7 compare_and_fusion
  8.6 1.8 gather_fusion
  10.6 0.7 and_select_fusion.2
  11.4 42.0 %psum.7 = f32[4,4]{1,0:T(4,128)S(1)} all-reduce(f32[4,4]{1,0:T(4,128)S(1)} %broadcast_select_fusion), channel_id=1, replica_groups=mesh['band'=4,'grid'=8] {'band','grid'}, use_global_device_ids=true, to_apply=%region_4.5 | all-reduce | flops 16 | bytes 128 | tf_op jit(solution)/shard_map/psum | solution.py:280
  53.4 0.2 fusion.31
  53.7 0.4 cholesky.15
  54.1 0.6 compare_reduce_fusion
  54.8 0.6 fusion.11
  55.4 0.3 custom-call.6
  55.8 0.7 broadcast_compare_fusion
  56.7 0.5 broadcast.243
  57.2 0.7 reduce.9
  58.0 0.7 fusion.28
  58.9 0.2 fusion.18
  59.2 0.7 fusion.30
  60.0 0.3 fusion.2.kern_ref
  60.4 5.5 %fusion.36.own_ref = f32[16,128,128]{2,1,0:T(8,128)S(1)} fusion(f32[4,16,128,128]{3,2,1,0:T(8,128)} %all-gather.4.cloned.1.call-done, f32[]{:T(128)} %bitcast.7, f32[]{:T(128)} %bitcast.6, f32[]{:T(128)} %bitcast.5, f32[]{:T(128)} %bitcast.4), kind=kLoop, calls=%fused_computation.72 | loop fusion | flops 1835008 | bytes 5242896 | tf_op jit(solution)/shard_map/add | solution.py:261
  65.9 5.5 %add_bitcast_fusion = (f32[16,128,128]{2,1,0:T(8,128)S(1)}, f32[16,128,128]{2,1,0:T(8,128)S(1)}) fusion(f32[4,16,128,128]{3,2,1,0:T(8,128)S(1)} %copy-done.2, f32[]{:T(128)} %bitcast.17, f32[]{:T(128)} %bitcast.16, f32[]{:T(128)} %bitcast.15, f32[]{:T(128)} %bitcast.14, f32[]{:T(128)} %bitcast.12, f32[]{:T(128)} %bitcast.11, f32[]{:T(128)} %bitcast.10, ...), kind=kLoop, calls=%fused_computation.15 | loop fusion | flops 3670016 | bytes 6291488 | tf_op jit(solution)/shard_map/add | solution.py:261
  71.5 99.3 %shard_map.68 = (f32[16,128,128]{2,1,0:T(8,128)S(1)}, f32[16,128,128]{2,1,0:T(8,128)}) custom-call(f32[16,128,128]{2,1,0:T(8,128)S(1)} %fusion.36.own_ref, f32[16,128,128]{2,1,0:T(8,128)S(1)} %get-tuple-element.12.first_ref, f32[16,128,128]{2,1,0:T(8,128)S(1)} %get-tuple-element.11.second_ref, f32[16,128,128]{2,1,0:T(8,128)S(1)} %fusion.2.kern_ref, ...), custom_call_target="tpu_custom_call" | custom-call | tf_op jit(solution)/shard_map/pallas_call | solution.py:224
  170.9 0.6 fusion.29
  171.5 6.1 %multiply_add_fusion = f32[1,16,128,128]{3,2,1,0:T(8,128)} fusion(f32[4,16,128,128]{3,2,1,0:T(8,128)} %all-gather.4.cloned.1.call-done, f32[]{:T(128)} %bitcast.7, f32[]{:T(128)} %bitcast.6, f32[]{:T(128)} %bitcast.5, f32[]{:T(128)} %bitcast.4), kind=kLoop, calls=%fused_computation.17 | loop fusion | flops 1835008 | bytes 5242896 | tf_op jit(solution)/shard_map/add | solution.py:261
  177.7 34.8 %all-gather.6.cloned.1.call-done = f32[64,128,128]{2,1,0:T(8,128)} async-done(((f32[16,128,128]{2,1,0:T(8,128)}), f32[64,128,128]{2,1,0:T(8,128)}) %all-gather.6.cloned.1.call-update) | async-done | bytes 4194320 | tf_op jit(solution)/shard_map/all_gather | solution.py:301
  212.5 6.1 %fusion.5 = f32[1,16,128,128]{3,2,1,0:T(8,128)} fusion(f32[16,128,128]{2,1,0:T(8,128)S(1)} %get-tuple-element.4, f32[64,128,128]{2,1,0:T(8,128)} %all-gather.6.cloned.1.call-done, f32[]{:T(128)} %bitcast.22, f32[]{:T(128)} %bitcast.21, f32[]{:T(128)} %bitcast.20, f32[]{:T(128)} %bitcast.19), kind=kLoop, calls=%fused_computation.9 | loop fusion | flops 2097152 | bytes 6291472 | tf_op jit(solution)/shard_map/broadcast_in_dim | solution.py:304
  (31 shorter events, 1.4 us)
Async XLA Ops:
  7.2 53.2 %all-gather.4.cloned.1.call-start = ((), (), s32[]{:S(2)}) async-start(), calls=%async_computation | async-start | bytes 5242880 | tf_op jit(solution)/shard_map/all_gather | solution.py:271
  7.9 204.6 %all-gather.6.cloned.1.call-start = ((), (), s32[]{:S(2)}) async-start(), calls=%async_computation.1 | async-start | bytes 5242880 | tf_op jit(solution)/shard_map/all_gather | solution.py:301
  60.4 5.5 %copy-start.2 = (f32[4,16,128,128]{3,2,1,0:T(8,128)S(1)}, f32[4,16,128,128]{3,2,1,0:T(8,128)}, u32[]{:S(2)}) copy-start(f32[4,16,128,128]{3,2,1,0:T(8,128)} %all-gather.4.cloned.1.call-done) | copy-start | bytes 12582916
  65.9 5.6 %copy-start = (f32[256,256]{1,0:T(8,128)S(1)}, f32[256,256]{1,0:T(8,128)}, u32[]{:S(2)}) copy-start(f32[256,256]{1,0:T(8,128)} %constant.137.clone.fwd_ref) | copy-start | bytes 786436
  65.9 5.6 %copy-start.1 = (f32[256,256]{1,0:T(8,128)S(1)}, f32[256,256]{1,0:T(8,128)}, u32[]{:S(2)}) copy-start(f32[256,256]{1,0:T(8,128)} %constant.138.clone.bwd_ref) | copy-start | bytes 786436
Sparse Core Ops, SparseCore 0:
  9.6 37.4 all-gather.3
  171.0 41.5 all-gather.5

commit v3 on v2

--- a/solution.py
+++ b/solution.py
@@ -35,14 +35,74 @@
     return jnp.dot(left, right, precision=precise, preferred_element_type=jnp.float32)
 
 
+def sum_kernel(n, bands, own_ref, out_ref, wide, from_grid, from_band, sems):
+    grid_me, band_me = lax.axis_index("grid"), lax.axis_index("band")
+    barrier = pltpu.get_barrier_semaphore()
+    axes = (("grid", n, grid_me), ("band", bands, band_me))
+    for axis, count, me in axes:
+        for step in range(1, count):
+            pl.semaphore_signal(
+                barrier, inc=1, device_id={axis: lax.rem(me + step, count)}, device_id_type=MESH
+            )
+    pl.semaphore_wait(barrier, n + bands - 2)
+    total = own_ref[...]
+    for place, (axis, count, me) in enumerate(axes):
+        wide[place] = total
+        landing = (from_grid, from_band)[place]
+        copies = []
+        for step in range(1, count):
+            copy = pltpu.make_async_remote_copy(
+                src_ref=wide.at[place],
+                dst_ref=landing.at[step],
+                send_sem=sems.at[place, 0, step],
+                recv_sem=sems.at[place, 1, step],
+                device_id={axis: lax.rem(me + step, count)},
+                device_id_type=MESH,
+            )
+            copy.start()
+            copies.append(copy)
+        for step, copy in enumerate(copies):
+            copy.wait()
+            total = total + landing[step + 1]
+    out_ref[...] = total
+
+
+def summed(table):
+    n, bands = lax.axis_size("grid"), lax.axis_size("band")
+    tile = (-(-table.shape[0] // 8) * 8, 128)
+    vmem = pl.BlockSpec(memory_space=pltpu.VMEM)
+    padded = jnp.pad(
+        table, ((0, tile[0] - table.shape[0]), (0, tile[1] - table.shape[1]))
+    )
+    result = pl.pallas_call(
+        functools.partial(sum_kernel, n, bands),
+        out_shape=jax.ShapeDtypeStruct(tile, jnp.float32),
+        in_specs=[vmem],
+        out_specs=vmem,
+        scratch_shapes=[
+            pltpu.VMEM((2,) + tile, jnp.float32),
+            pltpu.VMEM((n,) + tile, jnp.float32),
+            pltpu.VMEM((bands,) + tile, jnp.float32),
+            pltpu.SemaphoreType.DMA((2, 2, max(n, bands))),
+        ],
+        compiler_params=pltpu.CompilerParams(collective_id=1, has_side_effects=True),
+    )(padded)
+    return result[: table.shape[0], : table.shape[1]]
+
+
 def transform_kernel(
-    n, halves, chunks,
-    own_ref, first_ref, second_ref, kern_ref, fwd_ref, bwd_ref,
-    term_ref, off_ref,
-    send_one, recv_one, send_two, recv_two,
-    sems_one_send, sems_one_recv, sems_two_send, sems_two_recv, sems_own,
+    n, halves, chunks, chips,
+    mix_ref, share_ref, every_ref, kern_ref, fwd_ref, bwd_ref,
+    own_ref, term_ref,
+    send_one, recv_one, send_two, recv_two, second_ref, off_ref, twin_ref, going, coming,
+    sems_one_send, sems_one_recv, sems_two_send, sems_two_recv, sems_own, sems_twin, sems_chip,
 ):
+    bands = every_ref.shape[0]
     planes, length = own_ref.shape[0], own_ref.shape[2]
+    band_me = lax.axis_index("band")
+    chip, core = band_me // 2, lax.rem(band_me, 2)
+    partner = chip * 2 + 1 - core
+    peers = [lax.rem(chip + step, chips) * 2 + core for step in range(1, chips)]
     depth = length // n
     rows = depth // halves
     chunk = planes // chunks
@@ -52,7 +112,9 @@
         pl.semaphore_signal(
             barrier, inc=1, device_id={"grid": lax.rem(me + step, n)}, device_id_type=MESH
         )
-    pl.semaphore_wait(barrier, n - 1)
+    for peer in [partner] + peers:
+        pl.semaphore_signal(barrier, inc=1, device_id={"band": peer}, device_id_type=MESH)
+    pl.semaphore_wait(barrier, n - 1 + chips)
 
     def out_copies(part, half):
         size = chunk * rows
@@ -80,17 +142,19 @@
             sems_own.at[half],
         )
 
-    def back_copies(half):
+    def back_copies(half, part):
         size = planes * rows
+        step_size = chunk * rows
         copies = []
         for step in range(1, n):
             target = lax.rem(me + step, n)
+            start = pl.multiple_of(target * size + part * step_size, step_size)
             copies.append(
                 pltpu.make_async_remote_copy(
-                    src_ref=send_two.at[half, :, pl.ds(pl.multiple_of(target * size, size), size), :],
-                    dst_ref=recv_two.at[half, me],
-                    send_sem=sems_two_send.at[half, step],
-                    recv_sem=sems_two_recv.at[half, step],
+                    src_ref=send_two.at[half, :, pl.ds(start, step_size), :],
+                    dst_ref=recv_two.at[half, me, :, pl.ds(part * step_size, step_size), :],
+                    send_sem=sems_two_send.at[part, half, step],
+                    recv_sem=sems_two_recv.at[part, half, step],
                     device_id={"grid": target},
                     device_id_type=MESH,
                 )
@@ -109,8 +173,15 @@
         pieces = []
         for which in range(2):
             plane = pair * 2 + which
-            own = own_ref[plane]
-            both = jnp.concatenate([own * own, first_ref[plane] * second_ref[plane]], axis=1)
+            values = [every_ref[band, plane] for band in range(bands)]
+            own, first, second = [
+                sum(mix_ref[kind, band] * values[band] for band in range(1, bands))
+                + mix_ref[kind, 0] * values[0]
+                for kind in range(3)
+            ]
+            own_ref[plane] = own
+            second_ref[plane] = second
+            both = jnp.concatenate([own * own, first * second], axis=1)
             spectrum = times(both, fwd_ref[...])
             pieces.append(
                 jnp.concatenate([spectrum[:, :length], spectrum[:, length:]], axis=0)
@@ -166,14 +237,58 @@
             return carry
 
         lax.fori_loop(0, rows // 2, columns, 0)
-        for copy in back_copies(half):
-            copy.start()
+        for part in range(chunks):
+            for copy in back_copies(half, part):
+                copy.start()
         own_back(half).start()
 
     for half in range(halves):
         own_back(half).wait()
-        for copy in back_copies(half):
-            copy.wait_recv()
+
+    def twin_copy(part):
+        place = pl.ds(part * chunk, chunk)
+        return pltpu.make_async_remote_copy(
+            src_ref=off_ref.at[place],
+            dst_ref=twin_ref.at[place],
+            send_sem=sems_twin.at[0, part],
+            recv_sem=sems_twin.at[1, part],
+            device_id={"band": partner},
+            device_id_type=MESH,
+        )
+
+    def chip_copies(part):
+        place = pl.ds(part * chunk, chunk)
+        return [
+            pltpu.make_async_remote_copy(
+                src_ref=going.at[step, place],
+                dst_ref=coming.at[step, place],
+                send_sem=sems_chip.at[0, part, step],
+                recv_sem=sems_chip.at[1, part, step],
+                device_id={"band": peer},
+                device_id_type=MESH,
+            )
+            for step, peer in enumerate(peers)
+        ]
+
+    def shared(part):
+        twin_copy(part).wait_recv()
+
+        def one(plane, carry):
+            mine, other = off_ref[plane], twin_ref[plane]
+            for step, peer in enumerate(peers):
+                going[step, plane] = (
+                    share_ref[band_me, peer] * mine + share_ref[partner, peer] * other
+                )
+            term_ref[plane] = (
+                term_ref[plane]
+                + share_ref[band_me, band_me] * mine
+                + share_ref[partner, band_me] * other
+            )
+            return carry
+
+        lax.fori_loop(part * chunk, (part + 1) * chunk, one, 0)
+        for copy in chip_copies(part):
+            copy.start()
 
     def home(pair, carry):
         pieces = []
@@ -200,18 +315,40 @@
             off_ref[plane] = potential[:, length:] * second_ref[plane]
         return carry
 
-    lax.fori_loop(0, planes // 2, home, 0)
+    for part in range(chunks):
+        for half in range(halves):
+            for copy in back_copies(half, part):
+                copy.wait_recv()
+        lax.fori_loop(part * chunk // 2, (part + 1) * chunk // 2, home, 0)
+        twin_copy(part).start()
+        if part > 0:
+            shared(part - 1)
+    shared(chunks - 1)
+
+    def last(plane, carry):
+        total = term_ref[plane]
+        for step in range(chips - 1):
+            total = total + coming[step, plane]
+        term_ref[plane] = total
+        return carry
+
+    for part in range(chunks):
+        for copy in chip_copies(part):
+            copy.wait()
+        lax.fori_loop(part * chunk, (part + 1) * chunk, last, 0)
+        twin_copy(part).wait_send()
     for half in range(halves):
         for part in range(chunks):
             for copy in out_copies(part, half):
                 copy.wait_send()
-        for copy in back_copies(half):
-            copy.wait_send()
-
-
-def terms_of(own, first, second, kernel):
+            for copy in back_copies(half, part):
+                copy.wait_send()
+
+
+def exchanged(mix, share, every, kernel):
     n = lax.axis_size("grid")
-    planes, length = own.shape[0], own.shape[2]
+    planes, length = every.shape[1], every.shape[3]
+    chips = lax.axis_size("band") // 2
     depth = length // n
     halves = 2 if depth % 16 == 0 else 1
     rows = depth // halves
@@ -219,28 +356,36 @@
     chunks = planes // chunk
     forward = complex_table(length)
     vmem = pl.BlockSpec(memory_space=pltpu.VMEM)
-    slab = jax.ShapeDtypeStruct(own.shape, jnp.float32)
+    smem = pl.BlockSpec(memory_space=pltpu.SMEM)
+    slab = jax.ShapeDtypeStruct(every.shape[1:], jnp.float32)
     block = planes * rows
     return pl.pallas_call(
-        functools.partial(transform_kernel, n, halves, chunks),
+        functools.partial(transform_kernel, n, halves, chunks, chips),
         out_shape=(slab, slab),
-        in_specs=[vmem] * 6,
+        in_specs=[smem] * 2 + [vmem] * 4,
         out_specs=(vmem, vmem),
         scratch_shapes=[
             pltpu.VMEM((n, halves, 2, block, length), jnp.float32),
             pltpu.VMEM((halves, 2, n * block, length), jnp.float32),
             pltpu.VMEM((halves, 2, n * block, length), jnp.float32),
             pltpu.VMEM((halves, n, 2, block, length), jnp.float32),
+            pltpu.VMEM(slab.shape, jnp.float32),
+            pltpu.VMEM(slab.shape, jnp.float32),
+            pltpu.VMEM(slab.shape, jnp.float32),
+            pltpu.VMEM((chips - 1,) + slab.shape, jnp.float32),
+            pltpu.VMEM((chips - 1,) + slab.shape, jnp.float32),
             pltpu.SemaphoreType.DMA((chunks, halves, n)),
             pltpu.SemaphoreType.DMA((chunks, halves, n)),
-            pltpu.SemaphoreType.DMA((halves, n)),
-            pltpu.SemaphoreType.DMA((halves, n)),
+            pltpu.SemaphoreType.DMA((chunks, halves, n)),
+            pltpu.SemaphoreType.DMA((chunks, halves, n)),
             pltpu.SemaphoreType.DMA((2 * halves,)),
+            pltpu.SemaphoreType.DMA((2, chunks)),
+            pltpu.SemaphoreType.DMA((2, chunks, max(chips - 1, 1))),
         ],
         compiler_params=pltpu.CompilerParams(
             collective_id=0, has_side_effects=True, vmem_limit_bytes=40 * 1024 * 1024
         ),
-    )(own, first, second, kernel, jnp.asarray(forward), jnp.asarray(forward.T.copy()))
+    )(mix, share, every, kernel, jnp.asarray(forward), jnp.asarray(forward.T.copy()))
 
 
 def assignment(pattern):
@@ -253,13 +398,6 @@
     firsts = jnp.any(chosen, axis=2).astype(jnp.float32)
     seconds = jnp.any(chosen, axis=1).astype(jnp.float32)
     return firsts, seconds
-
-
-def mixed(coefficients, bands):
-    total = coefficients[0] * bands[0]
-    for band in range(1, bands.shape[0]):
-        total = total + coefficients[band] * bands[band]
-    return total
 
 
 def local(orbitals, pivots, pattern):
@@ -277,9 +415,7 @@
     sampled = jnp.sum(jnp.where(lanes[None, :] == (cell % length)[:, None], rows, 0.0), axis=1)
     own = jnp.where(inside, sampled, 0.0)
     ids = jnp.arange(block_total, dtype=jnp.int32)
-    picked = lax.psum(
-        jnp.where(ids[:, None] == band_index, own[None, :], 0.0), ("band", "grid")
-    )
+    picked = summed(jnp.where(ids[:, None] == band_index, own[None, :], 0.0))
     gram_matrix = jnp.dot(picked.T, picked, precision=precise)
     factor = jnp.linalg.cholesky(gram_matrix)
     rotation = lax.linalg.triangular_solve(factor, picked.T, left_side=True, lower=True).T
@@ -292,15 +428,9 @@
         ]
     )
     coefficients = jnp.dot(selectors, rotation.T, precision=precise)
-    localized = mixed(coefficients[0], every)
-    first = mixed(coefficients[1], every)
-    second = mixed(coefficients[2], every)
     depth = length // lax.axis_size("grid")
     kernel = coulomb(length, grid_index * depth, depth)
-    own_term, off_term = terms_of(localized, first, second, kernel)
-    terms = lax.all_gather(off_term, "band", axis=0, tiled=False)
-    weights = lax.dynamic_index_in_dim(firsts, band_index, 1, keepdims=False)
-    exchange_term = own_term + mixed(weights, terms)
+    localized, exchange_term = exchanged(coefficients, firsts, every, kernel)
     return (localized[None], exchange_term[None])
 
 

time: 226 us -> 179 us (0.79)
  blocking collectives: 42 us -> 0 us
  Pallas kernels: 99.3 us -> 132 us
  other arithmetic: 29.7 us -> 6.5 us
  waiting for transfers between devices: 35.6 us -> 15 us
  local copies, waits for them, and re-layouts: 3.97 us -> 9.2 us
    psum x1 -> x0, blocking collectives: 42 us -> none  [local(): lax.psum(jnp.where(ids[:, None] == band_index, own[None, :], 0.0), ('band...]
    all_gather x1 -> x0, waiting for transfers between devices: 34.8 us -> none  [local(): terms = lax.all_gather(off_term, 'band', axis=0, tiled=False)]
    pallas_call x1 -> x2, Pallas kernels: 99.3 us -> 132 us  [the longest x1 119 us: exchanged(): pl.pallas_call(functools.partial(transform_kernel, n, halves, chunks, chi...]
    add x3 -> x0, other arithmetic: 17.2 us -> none  [mixed(): total = total + coefficients[band] * bands[band]]
    all_gather x1, waiting for transfers between devices: 0.02 us -> 14.3 us  [local(): every = lax.all_gather(orbitals, 'band', axis=0, tiled=True)]
    broadcast_in_dim x1 -> x0, other arithmetic: 6.1 us -> none  [local(): return (localized[None], exchange_term[None])]
    unnamed x6 -> x8, local copies, waits for them, and re-layouts: 0.02 us -> 6.03 us
  transfers between devices with their start and end apart: 2 -> 1, of which waited for: 1 -> 1; matrix products, arithmetic and copies ran while one was open for 8% -> 7% of each run, Pallas kernels for 0% -> 7%
where the time goes in v3:
time: 179 us
  Pallas kernels  132 us (74%)
  waiting for transfers between devices  15 us (8%)
  between operations  14.1 us (8%)
  local copies, waits for them, and re-layouts  9.2 us (5%)
  other arithmetic  6.5 us (4%)
  matrix products  1.97 us (1%)
    pallas_call x1, Pallas kernels, exchanged(): pl.pallas_call(functools.partial(transform_kernel, n, halves, chunks, chi...  119 us
    all_gather x1, waiting for transfers between devices, local(): every = lax.all_gather(orbitals, 'band', axis=0, tiled=True)  14.3 us
    pallas_call x1, Pallas kernels, summed(): pl.pallas_call(functools.partial(sum_kernel, n, bands), out_shape=jax.Sha...  13 us
    unnamed x8, local copies, waits for them, and re-layouts  6.03 us
  transfers between devices with their start and end apart: 1, of which 1 were waited for; matrix products, arithmetic and copies ran while one was open for 7% of the time, Pallas kernels for 7%

profile of v3, /device:TPU:0, one launch (start us, length us, event | category | flops | bytes accessed | tf_op | source)
XLA Modules:
  0.0 179.0 jit_solution(18140814117472862391)
XLA Ops:
  7.2 0.7 all-gather.2.cloned.1.call-update
  7.9 0.7 broadcast_compare_fusion
  8.9 0.5 broadcast.197
  9.4 0.7 reduce.9
  10.1 0.7 fusion.26
  11.0 0.7 compare_and_fusion
  11.7 1.8 gather_fusion
  13.7 0.7 and_select_fusion.2
  14.4 0.6 pad.4.own_ref
  15.0 13.0 %shard_map.68 = f32[8,128]{1,0:T(8,128)} custom-call(f32[8,128]{1,0:T(8,128)} %pad.4.own_ref), custom_call_target="tpu_custom_call" | custom-call | tf_op jit(solution)/shard_map/pallas_call | solution.py:77
  28.1 1.0 fusion.19
  29.1 0.4 cholesky.15
  29.5 0.6 compare_reduce_fusion
  30.2 0.6 fusion.6
  30.8 0.3 custom-call.6
  31.2 0.9 fusion.13
  32.3 0.4 fusion.2.kern_ref
  32.7 14.3 %all-gather.2.cloned.1.call-done.every_ref = f32[4,16,128,128]{3,2,1,0:T(8,128)} async-done(((f32[1,16,128,128]{3,2,1,0:T(8,128)}), f32[4,16,128,128]{3,2,1,0:T(8,128)}) %all-gather.2.cloned.1.call-update) | async-done | bytes 4194320 | tf_op jit(solution)/shard_map/all_gather | solution.py:409
  46.9 2.2 %copy-done = f32[4,16,128,128]{3,2,1,0:T(8,128)S(1)} copy-done((f32[4,16,128,128]{3,2,1,0:T(8,128)S(1)}, f32[4,16,128,128]{3,2,1,0:T(8,128)}, u32[]{:S(2)}) %copy-start) | copy-done | bytes 4194328
  49.1 0.9 copy-done.1
  50.1 0.9 copy-done.2
  51.0 119.1 %shard_map.69 = (f32[16,128,128]{2,1,0:T(8,128)S(1)}, f32[16,128,128]{2,1,0:T(8,128)S(1)}) custom-call(f32[3,4]{1,0:T(4,128)S(1)} %fusion.7.mix_ref, f32[4,4]{1,0:T(4,128)S(1)} %convert_element_type.43.share_ref, f32[4,16,128,128]{3,2,1,0:T(8,128)S(1)} %copy-done, f32[16,128,128]{2,1,0:T(8,128)S(1)} %fusion.2.kern_ref, f32[256,256]{1,0:T(8,128)S(1)} %copy-done.2, ...), custom_call_target="tpu_custom_call" | custom-call | tf_op jit(solution)/shard_map/pallas_call | solution.py:362
  170.2 1.0 copy.15
  171.2 1.0 copy.16
  (24 shorter events, 1.2 us)
Async XLA Ops:
  7.2 39.8 %all-gather.2.cloned.1.call-start = ((), (), s32[]{:S(2)}) async-start(), calls=%async_computation | async-start | bytes 5242880 | tf_op jit(solution)/shard_map/all_gather | solution.py:409
  46.9 2.2 %copy-start = (f32[4,16,128,128]{3,2,1,0:T(8,128)S(1)}, f32[4,16,128,128]{3,2,1,0:T(8,128)}, u32[]{:S(2)}) copy-start(f32[4,16,128,128]{3,2,1,0:T(8,128)} %all-gather.2.cloned.1.call-done.every_ref) | copy-start | bytes 12582916
  49.1 0.9 copy-start.1
  50.1 0.9 copy-start.2
Sparse Core Ops, SparseCore 0:
  9.6 37.3 all-gather.1

commit v4 on v3

--- a/solution.py
+++ b/solution.py
@@ -92,10 +92,10 @@
 
 def transform_kernel(
     n, halves, chunks, chips,
-    mix_ref, share_ref, every_ref, kern_ref, fwd_ref, bwd_ref,
+    mix_ref, share_ref, orbital_ref, kern_ref, fwd_ref, bwd_ref,
     own_ref, term_ref,
-    send_one, recv_one, send_two, recv_two, second_ref, off_ref, twin_ref, going, coming,
-    sems_one_send, sems_one_recv, sems_two_send, sems_two_recv, sems_own, sems_twin, sems_chip,
+    send_one, recv_one, send_two, recv_two, second_ref, off_ref, twin_ref, going, coming, every_ref,
+    sems_one_send, sems_one_recv, sems_two_send, sems_two_recv, sems_own, sems_twin, sems_chip, sems_in, sems_keep,
 ):
     bands = every_ref.shape[0]
     planes, length = own_ref.shape[0], own_ref.shape[2]
@@ -116,6 +116,37 @@
         pl.semaphore_signal(barrier, inc=1, device_id={"band": peer}, device_id_type=MESH)
     pl.semaphore_wait(barrier, n - 1 + chips)
 
+    def part_copy(source, band, part, slot, target):
+        place = pl.ds(part * chunk, chunk)
+        return pltpu.make_async_remote_copy(
+            src_ref=source.at[place],
+            dst_ref=every_ref.at[band, place],
+            send_sem=sems_in.at[0, part, slot],
+            recv_sem=sems_in.at[1, part, slot],
+            device_id={"band": target},
+            device_id_type=MESH,
+        )
+
+    def direct_copies(part):
+        return [
+            part_copy(orbital_ref, band_me, part, slot, target)
+            for slot, target in enumerate(peers + [partner])
+        ]
+
+    def passed_copies(part):
+        copies = []
+        for step in range(1, chips):
+            band = lax.rem(chip + chips - step, chips) * 2 + core
+            copies.append(part_copy(every_ref.at[band], band, part, chips - 1 + step, partner))
+        return copies
+
+    keep = pltpu.make_async_copy(orbital_ref, every_ref.at[band_me], sems_keep.at[0])
+    keep.start()
+    for part in range(min(2, chunks)):
+        for copy in direct_copies(part):
+            copy.start()
+    keep.wait()
+
     def out_copies(part, half):
         size = chunk * rows
         mine = pl.ds(pl.multiple_of(me * (planes * rows) + part * size, size), size)
@@ -198,11 +229,22 @@
         return carry
 
     for part in range(chunks):
+        for copy in direct_copies(part):
+            copy.wait_recv()
+        for copy in passed_copies(part):
+            copy.start()
+        if part + 2 < chunks:
+            for copy in direct_copies(part + 2):
+                copy.start()
+        for copy in passed_copies(part):
+            copy.wait_recv()
         lax.fori_loop(part * chunk // 2, (part + 1) * chunk // 2, ahead, 0)
         for copy in out_copies(part, 0):
             copy.start()
     for half in range(1, halves):
         for part in range(chunks):
+            for copy in out_copies(part, half - 1):
+                copy.wait_send()
             for copy in out_copies(part, half):
                 copy.start()
     for half in range(halves):
@@ -237,10 +279,22 @@
             return carry
 
         lax.fori_loop(0, rows // 2, columns, 0)
+        own_back(half).start()
+        if half < halves - 1:
+            for part in range(chunks):
+                for copy in back_copies(half, part):
+                    copy.start()
+    for half in range(halves - 1):
         for part in range(chunks):
             for copy in back_copies(half, part):
+                copy.wait_send()
+            if half == halves - 2 and part >= chunks - min(2, chunks):
+                for copy in back_copies(halves - 1, part - chunks + min(2, chunks)):
+                    copy.start()
+    if halves == 1:
+        for part in range(min(2, chunks)):
+            for copy in back_copies(0, part):
                 copy.start()
-        own_back(half).start()
 
     for half in range(halves):
         own_back(half).wait()
@@ -316,6 +370,11 @@
         return carry
 
     for part in range(chunks):
+        for copy in back_copies(halves - 1, part):
+            copy.wait_send()
+        if part + 2 < chunks:
+            for copy in back_copies(halves - 1, part + 2):
+                copy.start()
         for half in range(halves):
             for copy in back_copies(half, part):
                 copy.wait_recv()
@@ -337,17 +396,16 @@
             copy.wait()
         lax.fori_loop(part * chunk, (part + 1) * chunk, last, 0)
         twin_copy(part).wait_send()
-    for half in range(halves):
-        for part in range(chunks):
-            for copy in out_copies(part, half):
-                copy.wait_send()
-            for copy in back_copies(half, part):
-                copy.wait_send()
-
-
-def exchanged(mix, share, every, kernel):
+    for part in range(chunks):
+        for copy in out_copies(part, halves - 1):
+            copy.wait_send()
+        for copy in direct_copies(part) + passed_copies(part):
+            copy.wait_send()
+
+
+def exchanged(mix, share, orbital, kernel):
     n = lax.axis_size("grid")
-    planes, length = every.shape[1], every.shape[3]
+    planes, length = orbital.shape[0], orbital.shape[2]
     chips = lax.axis_size("band") // 2
     depth = length // n
     halves = 2 if depth % 16 == 0 else 1
@@ -357,7 +415,7 @@
     forward = complex_table(length)
     vmem = pl.BlockSpec(memory_space=pltpu.VMEM)
     smem = pl.BlockSpec(memory_space=pltpu.SMEM)
-    slab = jax.ShapeDtypeStruct(every.shape[1:], jnp.float32)
+    slab = jax.ShapeDtypeStruct(orbital.shape, jnp.float32)
     block = planes * rows
     return pl.pallas_call(
         functools.partial(transform_kernel, n, halves, chunks, chips),
@@ -374,6 +432,7 @@
             pltpu.VMEM(slab.shape, jnp.float32),
             pltpu.VMEM((chips - 1,) + slab.shape, jnp.float32),
             pltpu.VMEM((chips - 1,) + slab.shape, jnp.float32),
+            pltpu.VMEM((2 * chips,) + slab.shape, jnp.float32),
             pltpu.SemaphoreType.DMA((chunks, halves, n)),
             pltpu.SemaphoreType.DMA((chunks, halves, n)),
             pltpu.SemaphoreType.DMA((chunks, halves, n)),
@@ -381,11 +440,13 @@
             pltpu.SemaphoreType.DMA((2 * halves,)),
             pltpu.SemaphoreType.DMA((2, chunks)),
             pltpu.SemaphoreType.DMA((2, chunks, max(chips - 1, 1))),
+            pltpu.SemaphoreType.DMA((2, chunks, 2 * chips - 1)),
+            pltpu.SemaphoreType.DMA((1,)),
         ],
         compiler_params=pltpu.CompilerParams(
             collective_id=0, has_side_effects=True, vmem_limit_bytes=40 * 1024 * 1024
         ),
-    )(mix, share, every, kernel, jnp.asarray(forward), jnp.asarray(forward.T.copy()))
+    )(mix, share, orbital, kernel, jnp.asarray(forward), jnp.asarray(forward.T.copy()))
 
 
 def assignment(pattern):
@@ -406,7 +467,6 @@
     block_total = pattern.shape[0]
     grid_index = lax.axis_index("grid")
     band_index = lax.axis_index("band")
-    every = lax.all_gather(orbitals, "band", axis=0, tiled=True)
     local_cell = pivots - grid_index * (slab_planes * length * length)
     inside = (local_cell >= 0) & (local_cell < slab_planes * length * length)
     cell = jnp.clip(local_cell, 0, slab_planes * length * length - 1)
@@ -430,7 +490,7 @@
     coefficients = jnp.dot(selectors, rotation.T, precision=precise)
     depth = length // lax.axis_size("grid")
     kernel = coulomb(length, grid_index * depth, depth)
-    localized, exchange_term = exchanged(coefficients, firsts, every, kernel)
+    localized, exchange_term = exchanged(coefficients, firsts, orbitals[0], kernel)
     return (localized[None], exchange_term[None])
 
 

time: 179 us -> 156 us (0.87)
  waiting for transfers between devices: 15 us -> 0 us
  between operations: 14.1 us -> 0.77 us
  Pallas kernels: 132 us -> 139 us
  local copies, waits for them, and re-layouts: 9.2 us -> 7.01 us
    all_gather x1 -> x0, waiting for transfers between devices: 14.3 us -> none  [local(): every = lax.all_gather(orbitals, 'band', axis=0, tiled=True)]
    pallas_call x1, Pallas kernels: 119 us -> 126 us  [exchanged(): pl.pallas_call(functools.partial(transform_kernel, n, halves, chunks, chi...]
    unnamed x8, local copies, waits for them, and re-layouts: 6.03 us -> 3.84 us
  transfers between devices with their start and end apart: 1 -> 0, of which waited for: 1 -> 0; matrix products, arithmetic and copies ran while one was open for 7% -> 0% of each run, Pallas kernels for 7% -> 0%
where the time goes in v4:
time: 156 us; the launch traced here: 155 us
  Pallas kernels  139 us (89%)
  local copies, waits for them, and re-layouts  7.01 us (4%)
  other arithmetic  6.57 us (4%)
  matrix products  1.97 us (1%)
    pallas_call x1, Pallas kernels, exchanged(): pl.pallas_call(functools.partial(transform_kernel, n, halves, chunks, chi...  126 us
    pallas_call x1, Pallas kernels, summed(): pl.pallas_call(functools.partial(sum_kernel, n, bands), out_shape=jax.Sha...  13 us
    unnamed x8, local copies, waits for them, and re-layouts  3.84 us

profile of v4, /device:TPU:0, one launch (start us, length us, event | category | flops | bytes accessed | tf_op | source)
XLA Modules:
  0.0 155.3 jit_solution(9312031519559944840)
XLA Ops:
  0.7 0.8 compare_and_fusion
  1.5 0.7 broadcast_compare_fusion
  2.2 0.2 reduce-window_clone.1
  2.4 0.5 broadcast.197
  2.9 0.7 reduce.9
  3.7 0.7 fusion.26
  4.4 0.1 fusion.5
  4.6 1.8 %gather_fusion = f32[4,128]{1,0:T(4,128)S(1)} fusion(f32[2048,128]{1,0:T(8,128)} %bitcast.15, s32[1024]{0:T(1024)S(1)} %pad_clamp_fusion), kind=kCustom, calls=%fused_computation | custom fusion | bytes 4112 | tf_op jit(solution)/shard_map/jit(_take)/gather | solution.py:473
  6.4 0.2 select_reduce_fusion.1
  6.6 0.7 and_select_fusion.2
  7.3 0.6 pad.4.own_ref
  7.9 13.0 %shard_map.68 = f32[8,128]{1,0:T(8,128)} custom-call(f32[8,128]{1,0:T(8,128)} %pad.4.own_ref), custom_call_target="tpu_custom_call" | custom-call | tf_op jit(solution)/shard_map/pallas_call | solution.py:77
  20.9 0.9 fusion.19
  21.9 0.4 cholesky.15
  22.3 0.6 compare_reduce_fusion
  23.0 0.6 fusion.6
  23.6 0.3 custom-call.6
  24.0 0.9 fusion.13
  25.1 0.4 fusion.2.kern_ref
  25.5 0.9 copy-done.1
  26.4 0.9 copy-done.2
  27.4 126.0 %shard_map.69 = (f32[16,128,128]{2,1,0:T(8,128)S(1)}, f32[16,128,128]{2,1,0:T(8,128)S(1)}) custom-call(f32[3,4]{1,0:T(4,128)S(1)} %fusion.7.mix_ref, f32[4,4]{1,0:T(4,128)S(1)} %convert_element_type.43.share_ref, f32[16,128,128]{2,1,0:T(8,128)S(1)} %bitcast.16, f32[16,128,128]{2,1,0:T(8,128)S(1)} %fusion.2.kern_ref, f32[256,256]{1,0:T(8,128)S(1)} %copy-done.2, ...), custom_call_target="tpu_custom_call" | custom-call | tf_op jit(solution)/shard_map/pallas_call | solution.py:420
  153.4 1.0 copy.13
  154.3 1.0 copy.14
  (21 shorter events, 0.6 us)
Async XLA Ops:
  0.6 24.8 %copy-start = (f32[1,16,128,128]{3,2,1,0:T(8,128)S(1)}, f32[1,16,128,128]{3,2,1,0:T(8,128)}, u32[]{:S(2)}) copy-start(f32[1,16,128,128]{3,2,1,0:T(8,128)} %param.5) | copy-start | bytes 3145732
  25.4 1.0 copy-start.1
  26.4 0.9 copy-start.2

commit v5 on v4

--- a/solution.py
+++ b/solution.py
@@ -147,11 +147,13 @@
             copy.start()
     keep.wait()
 
+    farthest = sorted(range(1, n), key=lambda step: (-min(step, n - step), step))
+
     def out_copies(part, half):
         size = chunk * rows
         mine = pl.ds(pl.multiple_of(me * (planes * rows) + part * size, size), size)
         copies = []
-        for step in range(1, n):
+        for step in farthest:
             target = lax.rem(me + step, n)
             copies.append(
                 pltpu.make_async_remote_copy(
@@ -177,7 +179,7 @@
         size = planes * rows
         step_size = chunk * rows
         copies = []
-        for step in range(1, n):
+        for step in farthest:
             target = lax.rem(me + step, n)
             start = pl.multiple_of(target * size + part * step_size, step_size)
             copies.append(

time: 156 us -> 156 us (level)
  no operation moved by 1% of the time
where the time goes in v5:
time: 156 us
  Pallas kernels  139 us (89%)
  local copies, waits for them, and re-layouts  7.01 us (4%)
  other arithmetic  6.57 us (4%)
  matrix products  1.97 us (1%)
    pallas_call x1, Pallas kernels, exchanged(): pl.pallas_call(functools.partial(transform_kernel, n, halves, chunks, chi...  126 us
    pallas_call x1, Pallas kernels, summed(): pl.pallas_call(functools.partial(sum_kernel, n, bands), out_shape=jax.Sha...  13 us
    unnamed x8, local copies, waits for them, and re-layouts  3.84 us

profile of v5, /device:TPU:0, one launch (start us, length us, event | category | flops | bytes accessed | tf_op | source)
XLA Modules:
  0.0 155.7 jit_solution(10293509555904450696)
XLA Ops:
  0.7 0.8 compare_and_fusion
  1.5 0.7 broadcast_compare_fusion
  2.2 0.2 reduce-window_clone.1
  2.4 0.5 broadcast.197
  2.9 0.7 reduce.9
  3.7 0.7 fusion.26
  4.4 0.1 fusion.5
  4.6 1.8 %gather_fusion = f32[4,128]{1,0:T(4,128)S(1)} fusion(f32[2048,128]{1,0:T(8,128)} %bitcast.15, s32[1024]{0:T(1024)S(1)} %pad_clamp_fusion), kind=kCustom, calls=%fused_computation | custom fusion | bytes 4112 | tf_op jit(solution)/shard_map/jit(_take)/gather | solution.py:475
  6.4 0.2 select_reduce_fusion.1
  6.6 0.7 and_select_fusion.2
  7.3 0.6 pad.4.own_ref
  7.9 13.0 %shard_map.68 = f32[8,128]{1,0:T(8,128)} custom-call(f32[8,128]{1,0:T(8,128)} %pad.4.own_ref), custom_call_target="tpu_custom_call" | custom-call | tf_op jit(solution)/shard_map/pallas_call | solution.py:77
  20.9 0.9 fusion.19
  21.9 0.4 cholesky.15
  22.3 0.6 compare_reduce_fusion
  23.0 0.6 fusion.6
  23.6 0.3 custom-call.6
  24.0 0.9 fusion.13
  25.1 0.4 fusion.2.kern_ref
  25.5 0.9 copy-done.1
  26.4 0.9 copy-done.2
  27.4 126.4 %shard_map.69 = (f32[16,128,128]{2,1,0:T(8,128)S(1)}, f32[16,128,128]{2,1,0:T(8,128)S(1)}) custom-call(f32[3,4]{1,0:T(4,128)S(1)} %fusion.7.mix_ref, f32[4,4]{1,0:T(4,128)S(1)} %convert_element_type.43.share_ref, f32[16,128,128]{2,1,0:T(8,128)S(1)} %bitcast.16, f32[16,128,128]{2,1,0:T(8,128)S(1)} %fusion.2.kern_ref, f32[256,256]{1,0:T(8,128)S(1)} %copy-done.2, ...), custom_call_target="tpu_custom_call" | custom-call | tf_op jit(solution)/shard_map/pallas_call | solution.py:422
  153.8 1.0 copy.13
  154.8 1.0 copy.14
  (21 shorter events, 0.6 us)
Async XLA Ops:
  0.6 24.8 %copy-start = (f32[1,16,128,128]{3,2,1,0:T(8,128)S(1)}, f32[1,16,128,128]{3,2,1,0:T(8,128)}, u32[]{:S(2)}) copy-start(f32[1,16,128,128]{3,2,1,0:T(8,128)} %param.5) | copy-start | bytes 3145732
  25.4 1.0 copy-start.1
  26.4 0.9 copy-start.2

commit v6 on v4

--- a/solution.py
+++ b/solution.py
@@ -288,11 +288,11 @@
         for part in range(chunks):
             for copy in back_copies(half, part):
                 copy.wait_send()
-            if half == halves - 2 and part >= chunks - min(2, chunks):
-                for copy in back_copies(halves - 1, part - chunks + min(2, chunks)):
+            if half == halves - 2 and part >= chunks - min(3, chunks):
+                for copy in back_copies(halves - 1, part - chunks + min(3, chunks)):
                     copy.start()
     if halves == 1:
-        for part in range(min(2, chunks)):
+        for part in range(min(3, chunks)):
             for copy in back_copies(0, part):
                 copy.start()
 
@@ -372,8 +372,8 @@
     for part in range(chunks):
         for copy in back_copies(halves - 1, part):
             copy.wait_send()
-        if part + 2 < chunks:
-            for copy in back_copies(halves - 1, part + 2):
+        if part + 3 < chunks:
+            for copy in back_copies(halves - 1, part + 3):
                 copy.start()
         for half in range(halves):
             for copy in back_copies(half, part):

time: 156 us -> 159 us (1.019)
  Pallas kernels: 139 us -> 142 us
    pallas_call x1, Pallas kernels: 126 us -> 129 us  [exchanged(): pl.pallas_call(functools.partial(transform_kernel, n, halves, chunks, chi...]
where the time goes in v6:
time: 159 us; the launch traced here: 158 us
  Pallas kernels  142 us (89%)
  local copies, waits for them, and re-layouts  7.01 us (4%)
  other arithmetic  6.57 us (4%)
  matrix products  1.97 us (1%)
    pallas_call x1, Pallas kernels, exchanged(): pl.pallas_call(functools.partial(transform_kernel, n, halves, chunks, chi...  129 us
    pallas_call x1, Pallas kernels, summed(): pl.pallas_call(functools.partial(sum_kernel, n, bands), out_shape=jax.Sha...  13 us
    unnamed x8, local copies, waits for them, and re-layouts  3.84 us

profile of v6, /device:TPU:0, one launch (start us, length us, event | category | flops | bytes accessed | tf_op | source)
XLA Modules:
  0.0 158.1 jit_solution(8948623202668760054)
XLA Ops:
  0.7 0.8 compare_and_fusion
  1.5 0.7 broadcast_compare_fusion
  2.2 0.2 reduce-window_clone.1
  2.4 0.5 broadcast.197
  2.9 0.7 reduce.9
  3.7 0.7 fusion.26
  4.4 0.1 fusion.5
  4.6 1.8 %gather_fusion = f32[4,128]{1,0:T(4,128)S(1)} fusion(f32[2048,128]{1,0:T(8,128)} %bitcast.15, s32[1024]{0:T(1024)S(1)} %pad_clamp_fusion), kind=kCustom, calls=%fused_computation | custom fusion | bytes 4112 | tf_op jit(solution)/shard_map/jit(_take)/gather | solution.py:473
  6.4 0.2 select_reduce_fusion.1
  6.6 0.7 and_select_fusion.2
  7.3 0.6 pad.4.own_ref
  7.9 13.0 %shard_map.68 = f32[8,128]{1,0:T(8,128)} custom-call(f32[8,128]{1,0:T(8,128)} %pad.4.own_ref), custom_call_target="tpu_custom_call" | custom-call | tf_op jit(solution)/shard_map/pallas_call | solution.py:77
  20.9 0.9 fusion.19
  21.9 0.4 cholesky.15
  22.3 0.6 compare_reduce_fusion
  23.0 0.6 fusion.6
  23.6 0.3 custom-call.6
  24.0 0.9 fusion.13
  25.1 0.4 fusion.2.kern_ref
  25.5 0.9 copy-done.1
  26.4 0.9 copy-done.2
  27.4 128.8 %shard_map.69 = (f32[16,128,128]{2,1,0:T(8,128)S(1)}, f32[16,128,128]{2,1,0:T(8,128)S(1)}) custom-call(f32[3,4]{1,0:T(4,128)S(1)} %fusion.7.mix_ref, f32[4,4]{1,0:T(4,128)S(1)} %convert_element_type.43.share_ref, f32[16,128,128]{2,1,0:T(8,128)S(1)} %bitcast.16, f32[16,128,128]{2,1,0:T(8,128)S(1)} %fusion.2.kern_ref, f32[256,256]{1,0:T(8,128)S(1)} %copy-done.2, ...), custom_call_target="tpu_custom_call" | custom-call | tf_op jit(solution)/shard_map/pallas_call | solution.py:420
  156.2 1.0 copy.13
  157.1 1.0 copy.14
  (21 shorter events, 0.6 us)
Async XLA Ops:
  0.6 24.8 %copy-start = (f32[1,16,128,128]{3,2,1,0:T(8,128)S(1)}, f32[1,16,128,128]{3,2,1,0:T(8,128)}, u32[]{:S(2)}) copy-start(f32[1,16,128,128]{3,2,1,0:T(8,128)} %param.5) | copy-start | bytes 3145732
  25.4 1.0 copy-start.1
  26.4 0.9 copy-start.2
